TPU v7x, 256 devices: a whole 4x4x8 slice. The times are simulated.
256 devices in a mesh: tgt: 4 (over z_lo, core), sup: 64 (over y, x, z_hi).
Axes of the slice: x: 4, y: 4, z: 8 (z_hi: 4, z_lo: 2; z = z_hi * 2 + z_lo), core: 2. Of those that a mesh axis runs over, the one named last changes fastest.
Arguments:
- support_images: bfloat16 [512, 3072], P('sup'), may hold values from -6 to 6
- target_images: bfloat16 [262144, 3072], P(('tgt', 'sup')), may hold values from -6 to 6
- support_labels: int32 [512], replicated, may hold values from 0 to 99
- target_labels: int32 [262144], P(('tgt', 'sup')), may hold values from 0 to 99
Outputs:
- scaled_grad: float32 [512, 3072], P('sup')
- loss: float32 [], replicated
All inputs are finite; a program needn't handle non-finite values.
Results may differ from a plain program's by a relative error of at most 0.0095.
Values may be sent and summed in bfloat16 or wider, within the bound.
A program may use at most 128 MiB of HBM per device.

v0:
```python
import math

import jax
import jax.numpy as jnp
from jax import lax
from jax.sharding import PartitionSpec as P

D = 3072
C = 100
LAYERS = 5


ridge_scale = 0.1
two_over_pi = 2.0 / math.pi


def ntk_kernel(gram_in, norm_row, norm_col):
    tangent = gram_in
    for layer_no in range(LAYERS):
        spread = (1.0 + 2.0 * norm_row) * (1.0 + 2.0 * norm_col)
        new_gram = two_over_pi * jnp.arcsin(2.0 * gram_in / jnp.sqrt(spread))
        slope_term = 2.0 * two_over_pi / jnp.sqrt(spread - 4.0 * gram_in * gram_in)
        tangent = new_gram + tangent * slope_term
        norm_row = two_over_pi * jnp.arcsin(2.0 * norm_row / (1.0 + 2.0 * norm_row))
        norm_col = two_over_pi * jnp.arcsin(2.0 * norm_col / (1.0 + 2.0 * norm_col))
        gram_in = new_gram
    return tangent


def ridge_solve(factor, rhs_block):
    middle = lax.linalg.triangular_solve(factor, rhs_block, left_side=True, lower=True)
    return lax.linalg.triangular_solve(factor, middle, left_side=True, lower=True, transpose_a=True)


def make_terms(
    coef_ts, coef_ss, target_images, support_images, rows_sup, column_scale, first_group
):
    back_dims = (((0,), (0,)), ((), ()))

    def term_rows(start, row_count):
        result = lax.dot_general(
            coef_ts, target_images, back_dims, preferred_element_type=jnp.float32
        )
        result = result + first_group * lax.dot_general(
            coef_ss, support_images, back_dims, preferred_element_type=jnp.float32
        )
        return result + column_scale[:, None] * rows_sup.astype(jnp.float32)

    return term_rows


def body(support_images, target_images, support_labels, target_labels):
    sup_rows = support_images.shape[0]
    tgt_rows = target_images.shape[0]
    n_sup = lax.axis_size("sup")
    n_tgt = lax.axis_size("tgt")
    total_sup = sup_rows * n_sup
    total_tgt = tgt_rows * n_sup * n_tgt
    contract = (((1,), (1,)), ((), ()))
    gathered = lax.all_gather(support_images, "sup", axis=0, tiled=True)
    norm_all = jnp.sum(jnp.square(gathered.astype(jnp.float32)), axis=1) / D
    norm_own = jnp.sum(jnp.square(support_images.astype(jnp.float32)), axis=1) / D
    norm_tgt = jnp.sum(jnp.square(target_images.astype(jnp.float32)), axis=1) / D
    gram_ts = (
        lax.dot_general(target_images, gathered, contract, preferred_element_type=jnp.float32) / D
    )
    gram_ss = (
        lax.dot_general(support_images, gathered, contract, preferred_element_type=jnp.float32) / D
    )
    kern_ts, pull_ts = jax.vjp(ntk_kernel, gram_ts, norm_tgt[:, None], norm_all[None, :])
    kern_own, pull_ss = jax.vjp(ntk_kernel, gram_ss, norm_own[:, None], norm_all[None, :])
    kern_ss = lax.all_gather(kern_own, "sup", axis=0, tiled=True)
    trace_mean = jnp.trace(kern_ss) / total_sup
    system = kern_ss + ridge_scale * trace_mean * jnp.eye(total_sup, dtype=jnp.float32)
    factor = jnp.linalg.cholesky(system)
    classes = jnp.arange(C, dtype=jnp.int32)
    label_sup = (support_labels[:, None] == classes[None, :]).astype(jnp.float32) - 1.0 / C
    label_tgt = (target_labels[:, None] == classes[None, :]).astype(jnp.float32) - 1.0 / C
    coeffs = ridge_solve(factor, label_sup)
    misfit = jnp.dot(kern_ts, coeffs, precision=lax.Precision.HIGHEST) - label_tgt
    loss_part = jnp.sum(misfit * misfit) / (2.0 * total_tgt)
    d_predict = misfit / total_tgt
    d_coeff_part = jnp.dot(kern_ts.T, d_predict, precision=lax.Precision.HIGHEST)
    d_coeffs, loss_value = lax.psum((d_coeff_part, loss_part), ("tgt", "sup"))
    adjoint = ridge_solve(factor, d_coeffs)
    ridge_grad = -ridge_scale / total_sup * jnp.sum(adjoint * coeffs)
    start_own = lax.axis_index("sup") * sup_rows
    adjoint_own = lax.dynamic_slice_in_dim(adjoint, start_own, sup_rows, 0)
    row_ids = start_own + jnp.arange(sup_rows, dtype=jnp.int32)
    col_ids = jnp.arange(total_sup, dtype=jnp.int32)
    diagonal = (row_ids[:, None] == col_ids[None, :]).astype(jnp.float32)
    d_kern_own = (
        -jnp.dot(adjoint_own, coeffs.T, precision=lax.Precision.HIGHEST) + ridge_grad * diagonal
    )
    d_kern_ts = jnp.dot(d_predict, coeffs.T, precision=lax.Precision.HIGHEST)
    g_ts, unused_tgt, qcol_ts = pull_ts(d_kern_ts)
    g_ss, qrow_ss, qcol_ss = pull_ss(d_kern_own)
    first_group = (lax.axis_index("tgt") == 0).astype(jnp.float32)
    coef_ts = (g_ts / D).astype(jnp.bfloat16)
    coef_ss = (g_ss / D).astype(jnp.bfloat16)
    column_scale = 2.0 / D * (qcol_ts[0] + first_group * qcol_ss[0])
    term_rows = make_terms(
        coef_ts, coef_ss, target_images, support_images, gathered, column_scale, first_group
    )
    partial_rows = lax.psum_scatter(
        term_rows(jnp.int32(0), sup_rows * lax.axis_size("sup")),
        "sup",
        scatter_dimension=0,
        tiled=True,
    )
    summed = lax.psum(partial_rows, "tgt")
    local_rows = jnp.dot(coef_ss, gathered, preferred_element_type=jnp.float32)
    local_rows = local_rows + 2.0 / D * qrow_ss * support_images.astype(jnp.float32)
    return (total_sup * (summed + local_rows), loss_value)


def solution(mesh):
    in_specs = (P("sup", None), P(("tgt", "sup"), None), P(), P(("tgt", "sup")))
    out_specs = (P("sup", None), P())
    return jax.shard_map(body, mesh=mesh, in_specs=in_specs, out_specs=out_specs, check_vma=False)
```

profile of v0, /device:TPU:1, one launch (start us, length us, event | category | flops | bytes accessed | tf_op | source)
XLA Modules:
  0.0 937.1 jit_solution(4720406489037573649)
XLA Ops:
  10.6 4.1 multiply_reduce_fusion
  15.8 82.0 %all-gather.3.cloned.1.call-done = bf16[512,3072]{1,0:T(8,128)(2,1)} async-done(((bf16[8,3072]{1,0:T(8,128)(2,1)}), bf16[512,3072]{1,0:T(8,128)(2,1)}) %all-gather.3.cloned.1.call-update) | async-done | bytes 3145744 | tf_op jit(solution)/shard_map/all_gather | solution.py:60
  97.8 2.7 fusion
  101.4 1.8 multiply_add_fusion.5
  103.5 36.9 %multiply_add_fusion = (f32[1024,512]{1,0:T(8,128)}, f32[1024,512]{1,0:T(8,128)}, f32[1024,512]{1,0:T(8,128)}, f32[1024,512]{1,0:T(8,128)}) fusion(f32[512]{0:T(512)S(1)} %get-tuple-element.154, f32[1024]{0:T(1024)S(1)} %multiply_add_fusion.10, f32[512]{0:T(512)S(1)} %get-tuple-element.119, f32[1024]{0:T(1024)S(1)} %get-tuple-element.135, ...), kind=kOutput, calls=%fused_computation.109 | convolution fusion | flops 3261071360 | bytes 17856512 | tf_op jit(solution)/shard_map/dot_general | solution.py:65
  140.5 35.2 %all-gather.5.cloned.1.call-done = f32[512,512]{1,0:T(8,128)} async-done(((f32[8,512]{1,0:T(8,128)}), f32[512,512]{1,0:T(8,128)}) %all-gather.5.cloned.1.call-update) | async-done | bytes 1048592 | tf_op jit(solution)/shard_map/all_gather | solution.py:72
  175.7 2.5 copy.23
  178.2 1.9 select_reduce_fusion
  180.8 2.3 select_add_fusion
  183.1 2.6 copy.24
  185.7 1.8 fusion.99
  188.5 11.7 %cholesky.103 = f32[128,128]{1,0:T(8,128)S(1)} custom-call(f32[128,128]{1,0:T(8,128)S(1)} %cholesky.263), custom_call_target="Cholesky" | custom-call | tf_op jit(solution)/shard_map/jit(cholesky)/cholesky | solution.py:75
  200.9 9.8 %custom-call.33 = f32[1,128,128]{1,2,0:T(8,128)S(1)} custom-call(f32[1,128,128]{2,1,0:T(8,128)S(1)} %get-tuple-element.131), custom_call_target="InvertDiagBlocksLowerTriangular" | custom-call | tf_op jit(solution)/shard_map/jit(cholesky)/cholesky | solution.py:75
  213.9 11.7 %cholesky.215 = f32[128,128]{1,0:T(8,128)S(1)} custom-call(f32[128,128]{1,0:T(8,128)S(1)} %cholesky.267), custom_call_target="Cholesky" | custom-call | tf_op jit(solution)/shard_map/jit(cholesky)/cholesky | solution.py:75
  229.6 11.0 %custom-call.34 = f32[1,128,128]{1,2,0:T(8,128)S(1)} custom-call(f32[1,128,128]{2,1,0:T(8,128)} %get-tuple-element.129), custom_call_target="InvertDiagBlocksLowerTriangular" | custom-call | tf_op jit(solution)/shard_map/jit(cholesky)/cholesky | solution.py:75
  241.4 1.5 constant_dynamic-update-slice_fusion.2
  242.8 1.9 convolution_dynamic-update-slice_fusion
  244.7 1.6 convolution_subtract_fusion.2
  246.4 11.7 %cholesky.236 = f32[128,128]{1,0:T(8,128)S(1)} custom-call(f32[128,128]{1,0:T(8,128)S(1)} %cholesky.272), custom_call_target="Cholesky" | custom-call | tf_op jit(solution)/shard_map/jit(cholesky)/cholesky | solution.py:75
  258.9 9.8 %custom-call.35 = f32[1,128,128]{1,2,0:T(8,128)S(1)} custom-call(f32[1,128,128]{2,1,0:T(8,128)S(1)} %get-tuple-element.127), custom_call_target="InvertDiagBlocksLowerTriangular" | custom-call | tf_op jit(solution)/shard_map/jit(cholesky)/cholesky | solution.py:75
  269.6 1.5 convolution_subtract_fusion.6
  271.1 11.9 %cholesky.253 = f32[128,128]{1,0:T(8,128)S(1)} custom-call(f32[128,128]{1,0:T(8,128)S(1)} %convolution_subtract_fusion.6), custom_call_target="Cholesky" | custom-call | tf_op jit(solution)/shard_map/jit(cholesky)/cholesky | solution.py:75
  288.9 2.4 select_select_fusion
  291.3 14.5 %while.8 = (s32[]{:T(128)}, f32[512,512]{0,1:T(8,128)}, s32[4,2]{0,1:T(2,128)S(1)}, f32[4,128,128]{2,1,0:T(8,128)}, s32[]{:T(128)}) while((s32[]{:T(128)}, f32[512,512]{0,1:T(8,128)}, s32[4,2]{0,1:T(2,128)S(1)}, f32[4,128,128]{2,1,0:T(8,128)}, s32[]{:T(128)}) %tuple.98), condition=%wide.while_cond.1, body=%wide.while_body.1.sunk | while | flops 2 | bytes 393829 | solution.py:32
  291.9 2.3 dynamic-slice.14
  295.6 2.3 dynamic-slice.14
  299.2 2.3 dynamic-slice.14
  302.8 2.2 dynamic-slice.14
  305.7 40.1 %custom-call.39 = f32[4,128,128]{1,2,0:T(8,128)S(1)} custom-call(f32[4,128,128]{2,1,0:T(8,128)} %get-tuple-element.33), custom_call_target="InvertDiagBlocksLowerTriangular" | custom-call | tf_op jit(solution)/shard_map/triangular_solve/custom-call.8 | solution.py:32
  345.9 1.3 fusion.155
  348.6 1.3 convolution_subtract_fusion.3
  350.2 1.4 convolution_subtract_fusion.5
  355.0 1.3 convolution_subtract_fusion.15
  356.7 2.8 multiply_reduce_fusion.1
  360.2 2.1 fusion.102
  362.5 18.7 %fusion.81 = (f32[1024,512]{1,0:T(8,128)S(1)}, f32[1024,512]{1,0:T(8,128)S(1)}, f32[1024,512]{1,0:T(8,128)S(1)}) fusion(f32[512]{0:T(512)} %copy-done.32, f32[1024]{0:T(1024)} %copy-done.50, f32[512]{0:T(512)S(1)} %copy-done.20, f32[1024]{0:T(1024)} %copy-done.38, f32[1024,512]{1,0:T(8,128)} %get-tuple-element.115, f32[512]{0:T(512)S(1)} %copy-done.22, ...), kind=kOutput, calls=%fused_computation.97 | convolution fusion | flops 658761728 | bytes 11118592 | tf_op jit(solution)/shard_map/dot_general | solution.py:95
  381.3 26.9 %fusion.92 = (f32[512]{0:T(512)}, f32[512]{0:T(512)}, f32[512]{0:T(512)}, f32[1024,512]{1,0:T(8,128)S(1)}, f32[1024,512]{1,0:T(8,128)S(1)}) fusion(f32[512]{0:T(512)S(1)} %copy-done.33, f32[1024]{0:T(1024)S(1)} %copy-done.51, f32[1024,512]{1,0:T(8,128)S(1)} %get-tuple-element.151, f32[1024,512]{1,0:T(8,128)S(1)} %copy-done.58, f32[512]{0:T(512)S(1)} %copy-done.20, ...), kind=kLoop, calls=%fused_computation.128 | loop fusion | flops 67107328 | bytes 16814080 | tf_op jit(solution)/shard_map/transpose(jvp())/reduce_sum | solution.py:20
  408.2 14.4 %fusion.61 = (f32[1024,512]{1,0:T(8,128)S(1)}, f32[1024,512]{1,0:T(8,128)S(1)}) fusion(f32[1024,512]{1,0:T(8,128)S(1)} %get-tuple-element.92, f32[1024,512]{1,0:T(8,128)S(1)} %get-tuple-element.91, f32[1024,512]{1,0:T(8,128)S(1)} %copy-done.4, f32[512]{0:T(512)S(1)} %copy-done.22, f32[1024]{0:T(1024)S(1)} %copy-done.37, f32[512]{0:T(512)S(1)} %copy-done.17, ...), kind=kLoop, calls=%fused_computation.77 | loop fusion | flops 24117248 | bytes 14704640 | tf_op jit(solution)/shard_map/transpose(jvp())/mul | solution.py:21
  422.6 12.5 %fusion.89 = (f32[512]{0:T(512)}, f32[512]{0:T(512)}, f32[1024,512]{1,0:T(8,128)S(1)}) fusion(f32[1024,512]{1,0:T(8,128)S(1)} %get-tuple-element.103, f32[512]{0:T(512)S(1)} %copy-done.17, f32[1024]{0:T(1024)S(1)} %copy-done.26, f32[1024,512]{1,0:T(8,128)S(1)} %get-tuple-element.104, f32[1024,512]{1,0:T(8,128)S(1)} %copy-done.2, f32[512]{0:T(512)S(1)} %copy-done.15, ...), kind=kLoop, calls=%fused_computation.125 | loop fusion | flops 36699136 | bytes 8404992 | tf_op jit(solution)/shard_map/transpose(jvp())/reduce_sum | solution.py:20
  435.1 14.1 %fusion.100 = f32[512,3072]{1,0:T(8,128)} fusion(bf16[1024,3072]{1,0:T(8,128)(2,1)S(1)} %bitcast.103, f32[1024,512]{1,0:T(8,128)S(1)} %get-tuple-element.93, f32[1024,512]{1,0:T(8,128)S(1)} %copy-done.2, f32[512]{0:T(512)S(1)} %copy-done.15, f32[1024]{0:T(1024)S(1)} %copy-done.24, f32[1024,512]{1,0:T(8,128)S(1)} %get-tuple-element.104, ...), kind=kOutput, calls=%fused_computation.161 | convolution fusion | flops 3242196992 | bytes 18886656 | tf_op jit(solution)/shard_map/dot_general | solution.py:41
  449.1 157.9 %all-reduce.4.cloned.1.call-done = f32[512,100]{0,1:T(8,128)} async-done(((f32[512,100]{0,1:T(8,128)}), f32[512,100]{0,1:T(8,128)}) %all-reduce.4.cloned.1.call-update) | async-done | bytes 204816 | tf_op jit(solution)/shard_map/psum | solution.py:84
  611.0 1.3 convolution_subtract_fusion.14
  615.6 1.3 convolution_subtract_fusion.13
  625.4 6.9 fusion.1
  633.1 78.1 %psum.23 = f32[]{:T(128)} all-reduce(f32[]{:T(128)S(6)} %div.757), channel_id=1, replica_groups=mesh['tgt'=4,'sup'=64] {'tgt','sup'}, use_global_device_ids=true, to_apply=%region_32.35 | all-reduce | flops 1 | bytes 8 | tf_op jit(solution)/shard_map/psum | solution.py:84
  711.2 174.7 %reduce-scatter.2.cloned.1.call-done = f32[8,3072]{1,0:T(8,128)} async-done(((f32[512,3072]{1,0:T(8,128)}), f32[8,3072]{1,0:T(8,128)}) %reduce-scatter.2.cloned.1.call-update) | async-done | bytes 98320 | tf_op jit(solution)/shard_map/reduce_scatter | solution.py:105
  886.0 42.1 %all-reduce.6.cloned.1.call-done = f32[8,3072]{1,0:T(8,128)} async-done(((f32[8,3072]{1,0:T(8,128)}), f32[8,3072]{1,0:T(8,128)}) %all-reduce.6.cloned.1.call-update) | async-done | bytes 98320 | tf_op jit(solution)/shard_map/psum | solution.py:111
  928.1 2.2 fusion.3
  (216 shorter events, 46.8 us)
Async XLA Ops:
  7.2 90.6 %all-gather.3.cloned.1.call-start = ((), (), s32[]{:S(2)}) async-start(), calls=%async_computation.1 | async-start | bytes 3194880 | tf_op jit(solution)/shard_map/all_gather | solution.py:60
  7.9 167.8 %all-gather.5.cloned.1.call-start = ((), (), s32[]{:S(2)}) async-start(), calls=%async_computation.2 | async-start | bytes 1064960 | tf_op jit(solution)/shard_map/all_gather | solution.py:72
  10.1 91.2 %copy-start.27 = (f32[8]{0:T(128)}, f32[8]{0:T(128)S(1)}, u32[]{:S(2)}) copy-start(f32[8]{0:T(128)S(1)} %get-tuple-element.148) | copy-start | bytes 100
  10.1 91.2 %copy-start.40 = (f32[8]{0:T(128)}, f32[8]{0:T(128)S(1)}, u32[]{:S(2)}) copy-start(f32[8]{0:T(128)S(1)} %get-tuple-element.110) | copy-start | bytes 100
  10.1 91.2 %copy-start.34 = (f32[8]{0:T(128)}, f32[8]{0:T(128)S(1)}, u32[]{:S(2)}) copy-start(f32[8]{0:T(128)S(1)} %broadcast_add_fusion.8) | copy-start | bytes 100
  10.6 90.7 %copy-start.41 = (f32[8]{0:T(128)}, f32[8]{0:T(128)S(1)}, u32[]{:S(2)}) copy-start(f32[8]{0:T(128)S(1)} %get-tuple-element.156) | copy-start | bytes 100
  10.6 90.7 %copy-start.48 = (f32[8]{0:T(128)}, f32[8]{0:T(128)S(1)}, u32[]{:S(2)}) copy-start(f32[8]{0:T(128)S(1)} %get-tuple-element.155) | copy-start | bytes 100
  14.7 86.6 %copy-start.6 = (bf16[8,3072]{1,0:T(8,128)(2,1)S(1)}, bf16[8,3072]{1,0:T(8,128)(2,1)}, u32[]{:S(2)}) copy-start(bf16[8,3072]{1,0:T(8,128)(2,1)} %param.8) | copy-start | bytes 147460
  14.9 88.5 %copy-start.23 = (f32[1024]{0:T(1024)}, f32[1024]{0:T(1024)S(1)}, u32[]{:S(2)}) copy-start(f32[1024]{0:T(1024)S(1)} %get-tuple-element.133) | copy-start | bytes 12292
  14.9 88.5 %copy-start.25 = (f32[1024]{0:T(1024)}, f32[1024]{0:T(1024)S(1)}, u32[]{:S(2)}) copy-start(f32[1024]{0:T(1024)S(1)} %get-tuple-element.137) | copy-start | bytes 12292
  14.9 88.5 %copy-start.36 = (f32[1024]{0:T(1024)}, f32[1024]{0:T(1024)S(1)}, u32[]{:S(2)}) copy-start(f32[1024]{0:T(1024)S(1)} %get-tuple-element.134) | copy-start | bytes 12292
  14.9 88.5 %copy-start.38 = (f32[1024]{0:T(1024)}, f32[1024]{0:T(1024)S(1)}, u32[]{:S(2)}) copy-start(f32[1024]{0:T(1024)S(1)} %get-tuple-element.135) | copy-start | bytes 12292
  15.0 88.5 %copy-start.50 = (f32[1024]{0:T(1024)}, f32[1024]{0:T(1024)S(1)}, u32[]{:S(2)}) copy-start(f32[1024]{0:T(1024)S(1)} %multiply_add_fusion.10) | copy-start | bytes 12292
  100.7 39.7 %copy-start.14 = (f32[512]{0:T(512)}, f32[512]{0:T(512)S(1)}, u32[]{:S(2)}) copy-start(f32[512]{0:T(512)S(1)} %get-tuple-element.145) | copy-start | bytes 6148
  100.7 39.7 %copy-start.19 = (f32[512]{0:T(512)}, f32[512]{0:T(512)S(1)}, u32[]{:S(2)}) copy-start(f32[512]{0:T(512)S(1)} %get-tuple-element.119) | copy-start | bytes 6148
  101.2 39.3 %copy-start.16 = (f32[512]{0:T(512)}, f32[512]{0:T(512)S(1)}, u32[]{:S(2)}) copy-start(f32[512]{0:T(512)S(1)} %get-tuple-element.146) | copy-start | bytes 6148
  101.2 39.3 %copy-start.21 = (f32[512]{0:T(512)}, f32[512]{0:T(512)S(1)}, u32[]{:S(2)}) copy-start(f32[512]{0:T(512)S(1)} %get-tuple-element.147) | copy-start | bytes 6148
  101.2 39.3 %copy-start.32 = (f32[512]{0:T(512)}, f32[512]{0:T(512)S(1)}, u32[]{:S(2)}) copy-start(f32[512]{0:T(512)S(1)} %get-tuple-element.154) | copy-start | bytes 6148
  103.2 503.8 %all-reduce.4.cloned.1.call-start = ((), (), s32[]{:S(2)}) async-start(), calls=%async_computation.3 | async-start | bytes 425984 | tf_op jit(solution)/shard_map/psum | solution.py:84
  241.3 41.8 %copy-start.56 = (f32[128]{0:T(128)S(1)}, f32[128]{0:T(128)}, u32[]{:S(2)}) copy-start(f32[128]{0:T(128)} %get-tuple-element.128) | copy-start | bytes 1540
  241.3 42.5 %copy-start.55 = (f32[128]{0:T(128)S(1)}, f32[128]{0:T(128)}, u32[]{:S(2)}) copy-start(f32[128]{0:T(128)} %get-tuple-element.130) | copy-start | bytes 1540
  244.7 46.6 %copy-start.57 = (s32[4]{0:T(128)S(1)}, s32[4]{0:T(128)}, u32[]{:S(2)}) copy-start(s32[4]{0:T(128)} %iota_multiply_fusion) | copy-start | bytes 52
  305.7 50.9 %copy-start.49 = (s32[1024]{0:T(1024)S(1)}, s32[1024]{0:T(1024)}, u32[]{:S(2)}) copy-start(s32[1024]{0:T(1024)} %param.11) | copy-start | bytes 12292
  345.9 10.8 %copy-start.1 = (f32[1024,512]{1,0:T(8,128)S(1)}, f32[1024,512]{1,0:T(8,128)}, u32[]{:S(2)}) copy-start(f32[1024,512]{1,0:T(8,128)} %get-tuple-element.114) | copy-start | bytes 6291460
  362.3 523.6 %reduce-scatter.2.cloned.1.call-start = ((), (), s32[]{:S(2)}) async-start(), calls=%async_computation.4 | async-start | bytes 6389760 | tf_op jit(solution)/shard_map/reduce_scatter | solution.py:105
  362.4 18.8 %copy-start.2 = (f32[1024,512]{1,0:T(8,128)S(1)}, f32[1024,512]{1,0:T(8,128)}, u32[]{:S(2)}) copy-start(f32[1024,512]{1,0:T(8,128)} %get-tuple-element.149) | copy-start | bytes 6291460
  362.4 18.8 %copy-start.4 = (f32[1024,512]{1,0:T(8,128)S(1)}, f32[1024,512]{1,0:T(8,128)}, u32[]{:S(2)}) copy-start(f32[1024,512]{1,0:T(8,128)} %get-tuple-element.116) | copy-start | bytes 6291460
  362.4 18.8 %copy-start.15 = (f32[512]{0:T(512)S(1)}, f32[512]{0:T(512)}, u32[]{:S(2)}) copy-start(f32[512]{0:T(512)} %copy-done.14) | copy-start | bytes 6148
  362.4 18.8 %copy-start.17 = (f32[512]{0:T(512)S(1)}, f32[512]{0:T(512)}, u32[]{:S(2)}) copy-start(f32[512]{0:T(512)} %copy-done.16) | copy-start | bytes 6148
  362.4 18.8 %copy-start.24 = (f32[1024]{0:T(1024)S(1)}, f32[1024]{0:T(1024)}, u32[]{:S(2)}) copy-start(f32[1024]{0:T(1024)} %copy-done.23) | copy-start | bytes 12292
  362.5 18.8 %copy-start.26 = (f32[1024]{0:T(1024)S(1)}, f32[1024]{0:T(1024)}, u32[]{:S(2)}) copy-start(f32[1024]{0:T(1024)} %copy-done.25) | copy-start | bytes 12292
  362.5 18.8 %copy-start.33 = (f32[512]{0:T(512)S(1)}, f32[512]{0:T(512)}, u32[]{:S(2)}) copy-start(f32[512]{0:T(512)} %copy-done.32) | copy-start | bytes 6148
  362.5 18.8 %copy-start.37 = (f32[1024]{0:T(1024)S(1)}, f32[1024]{0:T(1024)}, u32[]{:S(2)}) copy-start(f32[1024]{0:T(1024)} %copy-done.36) | copy-start | bytes 12292
  362.5 18.8 %copy-start.39 = (f32[1024]{0:T(1024)S(1)}, f32[1024]{0:T(1024)}, u32[]{:S(2)}) copy-start(f32[1024]{0:T(1024)} %copy-done.38) | copy-start | bytes 12292
  362.5 18.8 %copy-start.51 = (f32[1024]{0:T(1024)S(1)}, f32[1024]{0:T(1024)}, u32[]{:S(2)}) copy-start(f32[1024]{0:T(1024)} %copy-done.50) | copy-start | bytes 12292
  362.5 18.8 %copy-start.58 = (f32[1024,512]{1,0:T(8,128)S(1)}, f32[1024,512]{1,0:T(8,128)}, u32[]{:S(2)}) copy-start(f32[1024,512]{1,0:T(8,128)} %get-tuple-element.115) | copy-start | bytes 6291460
  381.3 53.8 %slice-start = ((s8[6291456]{0:T(1024)(128)(4,1)}), s8[4194304]{0:T(1024)(128)(4,1)S(1)}, s32[]{:S(2)}) async-start(s8[6291456]{0:T(1024)(128)(4,1)} %bitcast.102), calls=%async_computation.6 | async-start | bytes 8388608
  408.2 26.8 %slice-start.1 = ((s8[6291456]{0:T(1024)(128)(4,1)}), s8[2097152]{0:T(1024)(128)(4,1)S(1)}, s32[]{:S(2)}) async-start(s8[6291456]{0:T(1024)(128)(4,1)} %bitcast.102), calls=%async_computation.7 | async-start | bytes 4194304
  449.1 169.5 %copy-start.18 = (f32[8,512]{1,0:T(8,128)S(1)}, f32[8,512]{1,0:T(8,128)}, u32[]{:S(2)}) copy-start(f32[8,512]{1,0:T(8,128)} %get-tuple-element.109) | copy-start | bytes 49156
  607.0 10.2 %copy-start.12 = (f32[128,100]{0,1:T(8,128)S(1)}, f32[128,100]{0,1:T(8,128)}, u32[]{:S(2)}) copy-start(f32[128,100]{0,1:T(8,128)} %copy-done.11) | copy-start | bytes 153604
  632.4 253.6 %copy-start.43 = (f32[8]{0:T(128)S(1)}, f32[8]{0:T(128)}, u32[]{:S(2)}) copy-start(f32[8]{0:T(128)} %copy-done.42) | copy-start | bytes 100
  632.4 253.6 %copy-start.45 = (f32[8]{0:T(128)S(1)}, f32[8]{0:T(128)}, u32[]{:S(2)}) copy-start(f32[8]{0:T(128)} %copy-done.44) | copy-start | bytes 100
  632.4 253.6 %copy-start.47 = (f32[8]{0:T(128)S(1)}, f32[8]{0:T(128)}, u32[]{:S(2)}) copy-start(f32[8]{0:T(128)} %copy-done.46) | copy-start | bytes 100
  632.4 253.6 %copy-start.54 = (f32[8]{0:T(128)S(1)}, f32[8]{0:T(128)}, u32[]{:S(2)}) copy-start(f32[8]{0:T(128)} %copy-done.53) | copy-start | bytes 100
  632.4 295.8 %copy-start.7 = (bf16[8,3072]{1,0:T(8,128)(2,1)S(1)}, bf16[8,3072]{1,0:T(8,128)(2,1)}, u32[]{:S(2)}) copy-start(bf16[8,3072]{1,0:T(8,128)(2,1)} %param.8) | copy-start | bytes 147460
  632.4 295.8 %copy-start.28 = (f32[8]{0:T(128)S(1)}, f32[8]{0:T(128)}, u32[]{:S(2)}) copy-start(f32[8]{0:T(128)} %copy-done.27) | copy-start | bytes 100
  632.4 295.7 %copy-start.35 = (f32[8]{0:T(128)S(1)}, f32[8]{0:T(128)}, u32[]{:S(2)}) copy-start(f32[8]{0:T(128)} %copy-done.34) | copy-start | bytes 100
  632.4 295.7 %all-reduce.6.cloned.1.call-start = ((), (), s32[]{:S(2)}) async-start(), calls=%async_computation.5 | async-start | bytes 196608 | tf_op jit(solution)/shard_map/psum | solution.py:111
  (18 other events, 39.5 us)
Sparse Core Ops, SparseCore 0:
  11.3 86.4 all-gather.2
  103.3 72.3 all-gather.4
  362.5 244.4 all-reduce.3
  632.5 253.3 reduce-scatter.1
  888.5 39.5 all-reduce.5
where the time goes:
time: 942 us; the launch traced here: 937 us
  waiting for transfers between devices  493 us (52%)
  other arithmetic  201 us (21%)
  matrix products  116 us (12%)
  blocking collectives  78.1 us (8%)
  local copies, waits for them, and re-layouts  29.7 us (3%)
  between operations  19.5 us (2%)
    reduce_scatter x1, waiting for transfers between devices, body(): lax.psum_scatter(term_rows(jnp.int32(0), sup_rows * lax.axis_size('sup'))...  175 us
    psum x1, waiting for transfers between devices, body(): d_coeffs, loss_value = lax.psum((d_coeff_part, loss_part), ('tgt', 'sup'))  158 us
    another operation x15, other arithmetic, body(): factor = jnp.linalg.cholesky(system)  82 us
    all_gather x1, waiting for transfers between devices, body(): gathered = lax.all_gather(support_images, 'sup', axis=0, tiled=True)  82 us
    psum x1, blocking collectives, body(): d_coeffs, loss_value = lax.psum((d_coeff_part, loss_part), ('tgt', 'sup'))  78.1 us
    reduce_sum x7, other arithmetic, ntk_kernel(): spread = (1.0 + 2.0 * norm_row) * (1.0 + 2.0 * norm_col)  44.1 us
    another operation x4, other arithmetic, ridge_solve(): lax.linalg.triangular_solve(factor, middle, left_side=True, lower=True, t...  43.1 us
    psum x1, waiting for transfers between devices, body(): summed = lax.psum(partial_rows, 'tgt')  42.1 us
  transfers between devices with their start and end apart: 5, of which 5 were waited for; matrix products, arithmetic and copies ran while one was open for 14% of the time, Pallas kernels for 0%

commit v1 on v0

v1 whole, which is shorter than its diff:
```python
import functools
import math

import jax
import jax.numpy as jnp
from jax import lax
from jax.experimental import pallas as pl
from jax.experimental.pallas import tpu as pltpu
from jax.sharding import PartitionSpec as P

D = 3072
C = 100
LAYERS = 5
CLS = 128
RIDGE = 0.1
TWO_PI = 2.0 / math.pi
NEWTON = 7
REFINE = 3
HI = lax.Precision.HIGHEST
NN = (((1,), (0,)), ((), ()))
NT = (((1,), (1,)), ((), ()))
F32 = jnp.float32
BF16 = jnp.bfloat16

ASIN = (
    (1.0, 0.1666678637266159, 0.0749453455209732, 0.0455390103161335, 0.02390936389565468, 0.042553599923849106),
    (1.0, 0.16666781902313232, 0.07494797557592392, 0.04552660509943962, 0.02313542366027832, 0.0537058524787426, -0.05348314717411995, 0.08573318272829056),
    (1.0, 0.16666752099990845, 0.07495901733636856, 0.04535885155200958, 0.024863531813025475, 0.04080614075064659),
    (1.0, 0.16666492819786072, 0.0750882476568222, 0.043096426874399185, 0.04107564687728882),
    (1.0, 0.16666613519191742, 0.07503537833690643, 0.043817341327667236, 0.03804752230644226),
)


def poly(z, coefs):
    total = coefs[-1] * TWO_PI
    for value in coefs[-2::-1]:
        total = total * z + value * TWO_PI
    return total


def scaled_asin(layer, u, u2):
    if layer > 0:
        return u * poly(u2, ASIN[layer])
    size = jnp.abs(u)
    big = size > 0.5
    z = jnp.where(big, 0.5 - 0.5 * size, u2)
    s = jnp.where(big, z * lax.rsqrt(z), size)
    p = s * poly(z, ASIN[0])
    p = jnp.where(big, 1.0 - 2.0 * p, p)
    return jnp.where(u < 0.0, -p, p)


def norm_layers(p):
    scales, slopes = [], []
    chain = jnp.ones_like(p)
    for layer in range(LAYERS):
        spread = 1.0 + 2.0 * p
        inv = 1.0 / spread
        scales.append(lax.rsqrt(spread))
        slopes.append(chain * inv)
        if layer < LAYERS - 1:
            chain = chain * (2.0 * TWO_PI) * inv * lax.rsqrt(1.0 + 4.0 * p)
            u = 2.0 * p * inv
            p = scaled_asin(layer, u, u * u)
    return scales, slopes


def ntk_value(g, left, right):
    theta = g
    for layer in range(LAYERS):
        c2 = 2.0 * left[layer] * right[layer]
        u = g * c2
        u2 = u * u
        w = lax.rsqrt(1.0 - u2)
        g = scaled_asin(layer, u, u2)
        theta = g + theta * (TWO_PI * c2 * w)
    return theta


def ntk_full(g, left2, right, slope):
    theta = g
    dg = tg = gr = tr = None
    for layer in range(LAYERS):
        last = layer == LAYERS - 1
        c2 = left2[layer] * right[layer]
        u = g * c2
        u2 = u * u
        w = lax.rsqrt(1.0 - u2)
        cw2 = c2 * w
        step = TWO_PI * cw2
        bend = u * (w * cw2)
        ww = w * w
        tb = theta * bend
        gs = g * slope[layer]
        if layer == 0:
            tg_next = step * (2.0 + tb)
            dg_next = step
            base = -gs
            tr_next = step * (base - theta * (ww * slope[layer]))
        else:
            tg_next = step * (dg + tg + tb * dg)
            dg_next = step * dg
            base = gr - gs
            tr_next = step * (base + tr + (tb * gr - theta * (ww * slope[layer])))
        gr_next = step * base
        g = scaled_asin(layer, u, u2)
        theta = g + step * theta
        tg, dg, gr, tr = tg_next, dg_next, gr_next, tr_next
    return theta, tg, tr


def dot(a, b, dims=NN, precision=None):
    return lax.dot_general(a, b, dims, precision=precision, preferred_element_type=F32)


def split(x):
    high = x.astype(BF16)
    return high, (x - high.astype(F32)).astype(BF16)


def dot3(a, b, dims=NN):
    return dot(a[0], b[0], dims) + (dot(a[0], b[1], dims) + dot(a[1], b[0], dims))


def compute_kernel(
    lab_s, lab_t, sup, tgt,
    grad, slab, inv, system, coef_t, coef_n, own_tg, own_tr,
    gram, gram_ss, kern, tg_s, tr_s, coef, quant, quant_t, left_s, sq, mid, acc,
):
    n_sup = sup.shape[0]
    n_tgt = tgt.shape[0]
    total_tgt = n_tgt * lax.axis_size("sup") * lax.axis_size("tgt")
    own_rows = own_tg.shape[0]

    for j in range(n_sup // 256):
        gram_ss[:, j * 256:(j + 1) * 256] = dot(sup[...], sup[j * 256:(j + 1) * 256, :], NT) * (1.0 / D)

    def gram_tile(j, carry):
        rows = pl.ds(pl.multiple_of(j * 256, 256), 256)
        gram[:, rows] = dot(sup[...], tgt[rows, :], NT) * (1.0 / D)
        return carry

    lax.fori_loop(0, n_tgt // 256, gram_tile, 0)

    def square_tile(j, carry):
        rows = pl.ds(pl.multiple_of(j * 64, 64), 64)
        total = jnp.zeros((64, 128), F32)
        for k in range(D // 128):
            x = tgt[rows, k * 128:(k + 1) * 128].astype(F32)
            total = total + x * x
        sq[rows, :] = total
        return carry

    lax.fori_loop(0, n_tgt // 64, square_tile, 0)
    norm_t = dot(jnp.full((8, 128), 1.0 / D, F32), sq[...], NT, HI)
    scales_t, unused = norm_layers(norm_t)
    for layer in range(LAYERS):
        left_s[layer] = 2.0 * scales_t[layer]
    row_id = lax.broadcasted_iota(jnp.int32, (n_sup, n_sup), 0)
    col_id = lax.broadcasted_iota(jnp.int32, (n_sup, n_sup), 1)
    diagonal = row_id == col_id
    norm_s = jnp.sum(jnp.where(diagonal, gram_ss[...], 0.0), axis=0, keepdims=True)
    scales_s, slopes_s = norm_layers(jnp.broadcast_to(norm_s, (8, n_sup)))
    quant[...] = jnp.zeros_like(quant)
    for layer in range(LAYERS):
        quant[layer * 8:layer * 8 + 8, :] = scales_s[layer]
        quant[64 + layer * 8:72 + layer * 8, :] = slopes_s[layer]
    quant_t[...] = quant[...].T

    def ss_tile(i, carry):
        rows = pl.ds(pl.multiple_of(i * 8, 8), 8)
        q = quant_t[rows, :]
        left = [q[:, l * 8:l * 8 + 1] for l in range(LAYERS)]
        right = [quant[l * 8:l * 8 + 8, :] for l in range(LAYERS)]
        system[rows, :] = ntk_value(gram_ss[rows, :], left, right)
        return carry

    lax.fori_loop(0, n_sup // 8, ss_tile, 0)
    def own_tile(i, carry):
        here = pl.ds(pl.multiple_of(i * 8, 8), 8)
        own = pl.ds(pl.multiple_of(lax.axis_index("sup") * own_rows + i * 8, 8), 8)
        q = quant_t[own, :]
        left = [q[:, l * 8:l * 8 + 1] for l in range(LAYERS)]
        slope = [q[:, 64 + l * 8:65 + l * 8] for l in range(LAYERS)]
        right2 = [2.0 * quant[l * 8:l * 8 + 8, :] for l in range(LAYERS)]
        unused, tg, tr = ntk_full(gram_ss[own, :], right2, left, slope)
        own_tg[here, :] = tg
        own_tr[here, :] = tr
        return carry

    lax.fori_loop(0, own_rows // 8, own_tile, 0)

    half = 512

    def ts_tile(t, carry):
        i, j = t // (n_tgt // half), t % (n_tgt // half)
        rows = pl.ds(pl.multiple_of(i * 8, 8), 8)
        lanes = pl.ds(pl.multiple_of(j * half, half), half)
        q = quant_t[rows, :]
        right = [q[:, l * 8:l * 8 + 1] for l in range(LAYERS)]
        slope = [q[:, 64 + l * 8:65 + l * 8] for l in range(LAYERS)]
        left2 = [left_s[l, :, lanes] for l in range(LAYERS)]
        theta, tg, tr = ntk_full(gram[rows, lanes], left2, right, slope)
        kern[rows, lanes] = theta
        tg_s[rows, lanes] = tg
        tr_s[rows, lanes] = tr
        return carry

    lax.fori_loop(0, (n_sup // 8) * (n_tgt // half), ts_tile, 0)

    kern_ss = system[...]
    trace = jnp.sum(jnp.sum(jnp.where(diagonal, kern_ss, 0.0), axis=0, keepdims=True), axis=1, keepdims=True)
    inv_t = n_sup / trace
    system[...] = kern_ss * inv_t + jnp.where(diagonal, RIDGE, 0.0)
    norms = jnp.sum(jnp.abs(system[...]), axis=0, keepdims=True)
    high = jnp.minimum(jnp.max(norms, axis=1, keepdims=True), n_sup + RIDGE)
    alpha = 2.0 / (high + RIDGE)
    rho = (high - RIDGE) / (high + RIDGE)
    gain = 2.0 / (2.0 - rho * rho)
    inv[...] = (gain * alpha) * (jnp.where(diagonal, 2.0, 0.0) - alpha * system[...])
    rho = 0.5 * gain * rho * rho

    def newton(k, rho):
        a = split(system[...])
        x = split(inv[...])
        mid[...] = jnp.where(diagonal, 2.0, 0.0) - dot3(a, x)
        gain = 2.0 / (2.0 - rho * rho)
        inv[...] = gain * dot3(x, split(mid[...]))
        return 0.5 * gain * rho * rho

    lax.fori_loop(0, NEWTON, newton, rho)
    inv[...] = inv[...] * inv_t
    system[...] = system[...] * (trace * (1.0 / n_sup))

    class_id = lax.broadcasted_iota(jnp.int32, (CLS, n_sup), 0)
    label = jnp.where(class_id == lab_s[...], 1.0, 0.0) - 1.0 / C
    label = jnp.where(class_id < C, label, 0.0)
    coef_t[...] = dot(label, inv[...], NN, HI)
    for k in range(REFINE):
        left_over = label - dot(coef_t[...], system[...], NN, HI)
        coef_t[...] = coef_t[...] + dot(left_over, inv[...], NN, HI)
    coef_n[...] = coef_t[...].T

    class_id = lax.broadcasted_iota(jnp.int32, (CLS, n_tgt), 0)
    label = jnp.where(class_id == lab_t[...], 1.0, 0.0) - 1.0 / C
    label = jnp.where(class_id < C, label, 0.0)
    misfit = dot(coef_t[...], kern[...], NN, HI) - label
    loss = jnp.sum(jnp.sum(misfit * misfit, axis=0, keepdims=True), axis=1, keepdims=True) * (0.5 / total_tgt)
    d_predict = misfit * (1.0 / total_tgt)
    d_coef = dot(kern[...], d_predict, NT, HI)
    gram[...] = dot(coef_n[...], d_predict, NN, HI)

    def pull_tile(i, carry):
        rows = pl.ds(pl.multiple_of(i * 16, 16), 16)
        d_kern = gram[rows, :]
        coef[rows, :] = (d_kern * tg_s[rows, :] * (1.0 / D)).astype(BF16)
        through = d_kern * tr_s[rows, :]
        total = through[:, :128]
        for k in range(1, n_tgt // 128):
            total = total + through[:, k * 128:(k + 1) * 128]
        acc[rows, :] = total
        return carry

    lax.fori_loop(0, n_sup // 16, pull_tile, 0)
    d_norm = jnp.sum(acc[...], axis=1, keepdims=True)
    lane = lax.broadcasted_iota(jnp.int32, (n_sup, CLS), 1)
    d_coef = jnp.where(lane == C, loss, d_coef)
    slab[...] = jnp.where(lane == C + 1, d_norm, d_coef)

    def grad_tile(j, carry):
        lanes = pl.ds(pl.multiple_of(j * 512, 512), 512)
        grad[:, lanes] = dot(coef[...], tgt[:, lanes]).astype(grad.dtype)
        return carry

    lax.fori_loop(0, D // 512, grad_tile, 0)


def compute(gathered, target_images, lab_s, lab_t, own_rows, grad_type):
    n_sup, n_tgt = gathered.shape[0], target_images.shape[0]
    shapes = [
        ((n_sup, D), grad_type), ((n_sup, CLS), F32), ((n_sup, n_sup), F32), ((n_sup, n_sup), F32),
        ((CLS, n_sup), F32), ((n_sup, CLS), F32), ((own_rows, n_sup), F32), ((own_rows, n_sup), F32),
    ]
    vmem = pl.BlockSpec(memory_space=pltpu.VMEM)
    return pl.pallas_call(
        compute_kernel,
        out_shape=[jax.ShapeDtypeStruct(s, t) for s, t in shapes],
        in_specs=[vmem] * 4,
        out_specs=[vmem] * len(shapes),
        scratch_shapes=[
            pltpu.VMEM((n_sup, n_tgt), F32), pltpu.VMEM((n_sup, n_sup), F32),
            pltpu.VMEM((n_sup, n_tgt), F32), pltpu.VMEM((n_sup, n_tgt), F32), pltpu.VMEM((n_sup, n_tgt), F32),
            pltpu.VMEM((n_sup, n_tgt), BF16),
            pltpu.VMEM((128, n_sup), F32), pltpu.VMEM((n_sup, 128), F32),
            pltpu.VMEM((LAYERS, 8, n_tgt), F32), pltpu.VMEM((n_tgt, 128), F32),
            pltpu.VMEM((n_sup, n_sup), F32), pltpu.VMEM((n_sup, 128), F32),
        ],
        compiler_params=pltpu.CompilerParams(vmem_limit_bytes=56 * 2**20),
        name="compute",
    )(lab_s, lab_t, gathered, target_images)


def finish_kernel(sup, grad_own, total, inv, system, coef_t, coef_n, own_tg, own_tr, out, loss):
    n_sup = sup.shape[0]
    own_rows = grad_own.shape[0]
    start = pl.multiple_of(lax.axis_index("sup") * own_rows, 8)
    own = pl.ds(start, own_rows)
    lane = lax.broadcasted_iota(jnp.int32, (n_sup, CLS), 1)
    d_coef = jnp.where(lane < C, total[...], 0.0)
    adjoint = dot(inv[...], d_coef, NN, HI)
    for k in range(REFINE):
        left_over = d_coef - dot(system[...], adjoint, NN, HI)
        adjoint = adjoint + dot(inv[...], left_over, NN, HI)
    coefs = coef_n[...]
    ridge = jnp.sum(jnp.sum(adjoint * coefs, axis=0, keepdims=True), axis=1, keepdims=True) * (-RIDGE / n_sup)
    row_id = lax.broadcasted_iota(jnp.int32, (own_rows, n_sup), 0) + start
    col_id = lax.broadcasted_iota(jnp.int32, (own_rows, n_sup), 1)
    mine = row_id == col_id
    pick = jnp.where(mine, 1.0, 0.0)
    adj_own = dot(pick, adjoint, NN, HI)
    d_kern = jnp.where(mine, 2.0 * ridge, 0.0) - dot(adj_own, coef_t[...], NN, HI)
    d_kern = d_kern - dot(coef_n[own, :], adjoint, NT, HI)
    weight = d_kern * own_tg[...] * (1.0 / D)
    lane = lax.broadcasted_iota(jnp.int32, (own_rows, CLS), 1)
    slab_own = total[own, :]
    d_norm = jnp.sum(d_kern * own_tr[...], axis=1, keepdims=True)
    d_norm = d_norm + jnp.sum(jnp.where(lane == C + 1, slab_own, 0.0), axis=1, keepdims=True)
    loss[...] = jnp.where(lane == C, slab_own, 0.0)
    high, low = split(weight)
    for k in range(D // 512):
        lanes = slice(k * 512, (k + 1) * 512)
        part = dot(high, sup[:, lanes]) + dot(low, sup[:, lanes])
        part = part + grad_own[:, lanes].astype(F32)
        part = part + (2.0 / D) * d_norm * sup[own, lanes].astype(F32)
        out[:, lanes] = n_sup * part


def finish(gathered, grad_own, total, inv, system, coef_t, coef_n, own_tg, own_tr):
    own_rows = grad_own.shape[0]
    vmem = pl.BlockSpec(memory_space=pltpu.VMEM)
    return pl.pallas_call(
        finish_kernel,
        out_shape=[jax.ShapeDtypeStruct((own_rows, D), F32), jax.ShapeDtypeStruct((own_rows, CLS), F32)],
        in_specs=[vmem] * 9,
        out_specs=[vmem] * 2,
        compiler_params=pltpu.CompilerParams(vmem_limit_bytes=48 * 2**20),
        name="finish",
    )(gathered, grad_own, total, inv, system, coef_t, coef_n, own_tg, own_tr)


def body(support_images, target_images, support_labels, target_labels):
    own_rows = support_images.shape[0]
    lab_s = support_labels.reshape(1, -1)
    lab_t = target_labels.reshape(1, -1)
    gathered = lax.all_gather(support_images, "sup", axis=0, tiled=True)
    grad, slab, *rest = compute(gathered, target_images, lab_s, lab_t, own_rows, F32)
    total = lax.psum(slab, ("tgt", "sup"))
    grad_own = lax.psum(lax.psum_scatter(grad, "sup", scatter_dimension=0, tiled=True), "tgt")
    out, loss = finish(gathered, grad_own, total, *rest)
    return out, jnp.sum(loss[0])


def solution(mesh):
    in_specs = (P("sup", None), P(("tgt", "sup"), None), P(), P(("tgt", "sup")))
    out_specs = (P("sup", None), P())
    return jax.shard_map(body, mesh=mesh, in_specs=in_specs, out_specs=out_specs, check_vma=False)
```

time: 942 us -> 750 us (0.80)
  other arithmetic: 201 us -> 0.6 us
  waiting for transfers between devices: 493 us -> 640 us
  matrix products: 116 us -> 0 us
  Pallas kernels: 0 us -> 89.6 us
  blocking collectives: 78.1 us -> 0 us
  local copies, waits for them, and re-layouts: 29.7 us -> 5.25 us
    another operation x19 -> x0, other arithmetic: 125 us -> none  [the longest x15 82 us: body(): factor = jnp.linalg.cholesky(system)]
    psum x2, waiting for transfers between devices: 200 us -> 298 us  [the longest x1 254 us: body(): total = lax.psum(slab, ('tgt', 'sup'))]
    pallas_call x0 -> x2, Pallas kernels: none -> 89.6 us  [the longest x1 76.5 us: compute(): pl.pallas_call(compute_kernel, out_shape=[jax.ShapeDtypeStruct(s, t) for...]
    dot_general x9 -> x0, matrix products: 86.7 us -> none  [the longest x1 36.9 us: body(): lax.dot_general(target_images, gathered, contract, preferred_element_type...]
    psum x1 -> x0, blocking collectives: 78.1 us -> none  [body(): d_coeffs, loss_value = lax.psum((d_coeff_part, loss_part), ('tgt', 'sup'))]
    reduce_scatter x1, waiting for transfers between devices: 175 us -> 251 us  [body(): lax.psum_scatter(grad, 'sup', scatter_dimension=0, tiled=True)]
    reduce_sum x12 -> x1, other arithmetic: 54.5 us -> 0.6 us  [body(): return (out, jnp.sum(loss[0]))]
    all_gather x1 -> x0, waiting for transfers between devices: 35.2 us -> none  [body(): kern_ss = lax.all_gather(kern_own, 'sup', axis=0, tiled=True)]
  transfers between devices with their start and end apart: 5 -> 4, of which waited for: 5 -> 4; matrix products, arithmetic and copies ran while one was open for 14% -> 0% of each run, Pallas kernels for 0% -> 0%
where the time goes in v1:
time: 750 us
  waiting for transfers between devices  640 us (85%)
  Pallas kernels  89.6 us (12%)
  between operations  13.8 us (2%)
    psum x1, waiting for transfers between devices, body(): total = lax.psum(slab, ('tgt', 'sup'))  254 us
    reduce_scatter x1, waiting for transfers between devices, body(): lax.psum_scatter(grad, 'sup', scatter_dimension=0, tiled=True)  251 us
    all_gather x1, waiting for transfers between devices, body(): gathered = lax.all_gather(support_images, 'sup', axis=0, tiled=True)  89.9 us
    pallas_call x1, Pallas kernels, compute(): pl.pallas_call(compute_kernel, out_shape=[jax.ShapeDtypeStruct(s, t) for...  76.5 us
    psum x1, waiting for transfers between devices, body(): lax.psum(lax.psum_scatter(grad, 'sup', scatter_dimension=0, tiled=True),...  43.5 us
  transfers between devices with their start and end apart: 4, of which 4 were waited for; matrix products, arithmetic and copies ran while one was open for 0% of the time, Pallas kernels for 0%

profile of v1, /device:TPU:1, one launch (start us, length us, event | category | flops | bytes accessed | tf_op | source)
XLA Modules:
  0.0 749.6 jit_solution(9778930747671574292)
XLA Ops:
  7.2 0.0 all-gather.2.cloned.1.call-start
  7.2 0.7 all-gather.2.cloned.1.call-update
  7.9 0.0 reduce-scatter.2.cloned.1.call-start
  7.9 89.9 %all-gather.2.cloned.1.call-done.sup = bf16[512,3072]{1,0:T(8,128)(2,1)} async-done(((bf16[8,3072]{1,0:T(8,128)(2,1)}), bf16[512,3072]{1,0:T(8,128)(2,1)}) %all-gather.2.cloned.1.call-update) | async-done | bytes 3145744 | tf_op jit(solution)/shard_map/all_gather | solution.py:355
  97.8 0.0 copy-start
  97.8 76.5 %compute.1 = (f32[512,3072]{1,0:T(8,128)}, f32[512,128]{1,0:T(8,128)}, f32[512,512]{1,0:T(8,128)}, f32[512,512]{1,0:T(8,128)}, f32[128,512]{1,0:T(8,128)}, /*ind...) custom-call(s32[1,512]{1,0:T(1,128)} %bitcast.3, s32[1,1024]{1,0:T(1,128)} %bitcast.2, ...), custom_call_target="tpu_custom_call" | custom-call | tf_op jit(solution)/shard_map/compute/pallas_call | solution.py:285
  174.3 0.0 copy-start.3
  174.3 0.0 copy-start.7
  174.3 0.0 copy-start.8
  174.3 0.0 reduce-scatter.2.cloned.1.call-update
  174.3 0.0 all-reduce.5.cloned.1.call-start
  174.4 0.7 all-reduce.5.cloned.1.call-update
  175.1 0.0 all-reduce.3.cloned.1.call-start
  175.1 251.4 %reduce-scatter.2.cloned.1.call-done = f32[8,3072]{1,0:T(8,128)} async-done(((f32[512,3072]{1,0:T(8,128)}), f32[8,3072]{1,0:T(8,128)}) %reduce-scatter.2.cloned.1.call-update) | async-done | bytes 98320 | tf_op jit(solution)/shard_map/reduce_scatter | solution.py:358
  426.5 0.0 all-reduce.3.cloned.1.call-update
  426.6 254.1 %all-reduce.5.cloned.1.call-done.total = f32[512,128]{1,0:T(8,128)} async-done(((f32[512,128]{1,0:T(8,128)}), f32[512,128]{1,0:T(8,128)}) %all-reduce.5.cloned.1.call-update) | async-done | bytes 262160 | tf_op jit(solution)/shard_map/psum | solution.py:357
  680.6 43.5 %all-reduce.3.cloned.1.call-done.grad_own = f32[8,3072]{1,0:T(8,128)} async-done(((f32[8,3072]{1,0:T(8,128)}), f32[8,3072]{1,0:T(8,128)}) %all-reduce.3.cloned.1.call-update) | async-done | bytes 98320 | tf_op jit(solution)/shard_map/psum | solution.py:358
  724.1 0.0 copy-done
  724.1 0.0 copy-done.3
  724.1 0.0 copy-done.7
  724.1 0.0 copy-done.8
  724.1 0.0 copy-start.1
  724.1 1.2 copy-done.1
  725.3 0.0 copy-start.2
  725.3 1.2 copy-done.2
  726.6 0.0 copy-start.4
  726.6 0.9 copy-done.4
  727.5 0.0 copy-start.5
  727.5 0.9 copy-done.5
  728.5 0.0 copy-start.6
  728.5 0.9 copy-done.6
  729.4 13.2 %finish.1 = (f32[8,3072]{1,0:T(8,128)}, f32[8,128]{1,0:T(8,128)S(1)}) custom-call(bf16[512,3072]{1,0:T(8,128)(2,1)S(1)} %copy-done, f32[8,3072]{1,0:T(8,128)S(1)} %copy-done.6, f32[512,128]{1,0:T(8,128)S(1)} %copy-done.5, f32[512,512]{1,0:T(8,128)S(1)} %copy-done.1, f32[512,512]{1,0:T(8,128)S(1)} %copy-done.2, f32[128,512]{1,0:T(8,128)S(1)} %copy-done.3, ...), custom_call_target="tpu_custom_call" | custom-call | tf_op jit(solution)/shard_map/finish/pallas_call | solution.py:341
  742.5 0.6 slice_reduce_fusion
Async XLA Ops:
  7.2 90.6 %all-gather.2.cloned.1.call-start = ((), (), s32[]{:S(2)}) async-start(), calls=%async_computation.1 | async-start | bytes 3194880 | tf_op jit(solution)/shard_map/all_gather | solution.py:355
  7.9 418.6 %reduce-scatter.2.cloned.1.call-start = ((), (), s32[]{:S(2)}) async-start(), calls=%async_computation.2 | async-start | bytes 6389760 | tf_op jit(solution)/shard_map/reduce_scatter | solution.py:358
  97.8 626.3 %copy-start = (bf16[512,3072]{1,0:T(8,128)(2,1)S(1)}, bf16[512,3072]{1,0:T(8,128)(2,1)}, u32[]{:S(2)}) copy-start(bf16[512,3072]{1,0:T(8,128)(2,1)} %all-gather.2.cloned.1.call-done.sup) | copy-start | bytes 9437188
  174.3 549.8 %copy-start.3 = (f32[128,512]{1,0:T(8,128)S(1)}, f32[128,512]{1,0:T(8,128)}, u32[]{:S(2)}) copy-start(f32[128,512]{1,0:T(8,128)} %get-tuple-element.16.coef_t) | copy-start | bytes 786436
  174.3 549.8 %copy-start.7 = (f32[8,512]{1,0:T(8,128)S(1)}, f32[8,512]{1,0:T(8,128)}, u32[]{:S(2)}) copy-start(f32[8,512]{1,0:T(8,128)} %get-tuple-element.18.own_tg) | copy-start | bytes 49156
  174.3 549.8 %copy-start.8 = (f32[8,512]{1,0:T(8,128)S(1)}, f32[8,512]{1,0:T(8,128)}, u32[]{:S(2)}) copy-start(f32[8,512]{1,0:T(8,128)} %get-tuple-element.19.own_tr) | copy-start | bytes 49156
  174.3 506.3 %all-reduce.5.cloned.1.call-start = ((), (), s32[]{:S(2)}) async-start(), calls=%async_computation.4 | async-start | bytes 524288 | tf_op jit(solution)/shard_map/psum | solution.py:357
  175.1 549.0 %all-reduce.3.cloned.1.call-start = ((), (), s32[]{:S(2)}) async-start(), calls=%async_computation.3 | async-start | bytes 196608 | tf_op jit(solution)/shard_map/psum | solution.py:358
  724.1 1.2 copy-start.1
  725.3 1.2 copy-start.2
  726.6 0.9 copy-start.4
  727.5 0.9 copy-start.5
  728.5 0.9 copy-start.6
Sparse Core Ops, SparseCore 0:
  11.3 86.4 all-gather.1
  174.5 252.0 reduce-scatter.1
  432.9 247.6 all-reduce.4
  683.3 40.7 all-reduce.2

commit v2 on v1

--- a/solution.py
+++ b/solution.py
@@ -122,11 +122,27 @@
     return dot(a[0], b[0], dims) + (dot(a[0], b[1], dims) + dot(a[1], b[0], dims))
 
 
+def load_images(gathered, sup, sems):
+    half = D // 2
+    copies = []
+    for y in range(4):
+        for x in range(4):
+            rows = pl.ds(32 * (y * 4 + x), 32)
+            for h, slot in ((0, y * 4 + x), (1, x * 4 + y)):
+                dst = sup.at[rows, h * half:(h + 1) * half]
+                copies.append(pltpu.make_async_copy(gathered.at[h, slot], dst, sems.at[len(copies)]))
+    for copy in copies:
+        copy.start()
+    return copies
+
+
 def compute_kernel(
-    lab_s, lab_t, sup, tgt,
+    lab_s, lab_t, gathered, tgt,
     grad, slab, inv, system, coef_t, coef_n, own_tg, own_tr,
-    gram, gram_ss, kern, tg_s, tr_s, coef, quant, quant_t, left_s, sq, mid, acc,
+    sup, gram, gram_ss, kern, tg_s, tr_s, coef, quant, quant_t, left_s, sq, mid, acc, sems,
 ):
+    for copy in load_images(gathered, sup, sems):
+        copy.wait()
     n_sup = sup.shape[0]
     n_tgt = tgt.shape[0]
     total_tgt = n_tgt * lax.axis_size("sup") * lax.axis_size("tgt")
@@ -253,7 +269,11 @@
     def pull_tile(i, carry):
         rows = pl.ds(pl.multiple_of(i * 16, 16), 16)
         d_kern = gram[rows, :]
-        coef[rows, :] = (d_kern * tg_s[rows, :] * (1.0 / D)).astype(BF16)
+        part = (d_kern * tg_s[rows, :] * (1.0 / D)).astype(BF16)
+        coef[0, rows, :] = part
+        block = i // 2
+        other = (block % 4) * 4 + block // 4
+        coef[1, pl.ds(pl.multiple_of(other * 32 + (i % 2) * 16, 16), 16), :] = part
         through = d_kern * tr_s[rows, :]
         total = through[:, :128]
         for k in range(1, n_tgt // 128):
@@ -265,44 +285,53 @@
     d_norm = jnp.sum(acc[...], axis=1, keepdims=True)
     lane = lax.broadcasted_iota(jnp.int32, (n_sup, CLS), 1)
     d_coef = jnp.where(lane == C, loss, d_coef)
-    slab[...] = jnp.where(lane == C + 1, d_norm, d_coef)
-
-    def grad_tile(j, carry):
-        lanes = pl.ds(pl.multiple_of(j * 512, 512), 512)
-        grad[:, lanes] = dot(coef[...], tgt[:, lanes]).astype(grad.dtype)
-        return carry
-
-    lax.fori_loop(0, D // 512, grad_tile, 0)
-
-
-def compute(gathered, target_images, lab_s, lab_t, own_rows, grad_type):
-    n_sup, n_tgt = gathered.shape[0], target_images.shape[0]
+    acc[...] = jnp.where(lane == C + 1, d_norm, d_coef)
+    slab[0] = acc[...]
+    for y in range(4):
+        for x in range(4):
+            slab[1, 32 * (x * 4 + y):32 * (x * 4 + y) + 32, :] = acc[32 * (y * 4 + x):32 * (y * 4 + x) + 32, :]
+
+    for h in range(2):
+        def grad_tile(j, carry):
+            there = pl.ds(pl.multiple_of(j * 512, 512), 512)
+            lanes = pl.ds(pl.multiple_of(j * 512 + h * (D // 2), 512), 512)
+            grad[h, :, there] = dot(coef[h], tgt[:, lanes]).astype(grad.dtype)
+            return carry
+
+        lax.fori_loop(0, D // 1024, grad_tile, 0)
+
+
+def compute(gathered, target_images, lab_s, lab_t, own_rows):
+    n_sup, n_tgt = gathered.size // D, target_images.shape[0]
     shapes = [
-        ((n_sup, D), grad_type), ((n_sup, CLS), F32), ((n_sup, n_sup), F32), ((n_sup, n_sup), F32),
+        ((2, n_sup, D // 2), BF16), ((2, n_sup, CLS), F32), ((n_sup, n_sup), F32), ((n_sup, n_sup), F32),
         ((CLS, n_sup), F32), ((n_sup, CLS), F32), ((own_rows, n_sup), F32), ((own_rows, n_sup), F32),
     ]
     vmem = pl.BlockSpec(memory_space=pltpu.VMEM)
     return pl.pallas_call(
         compute_kernel,
         out_shape=[jax.ShapeDtypeStruct(s, t) for s, t in shapes],
-        in_specs=[vmem] * 4,
+        in_specs=[vmem, vmem, pl.BlockSpec(memory_space=pl.ANY), vmem],
         out_specs=[vmem] * len(shapes),
         scratch_shapes=[
+            pltpu.VMEM((n_sup, D), BF16),
             pltpu.VMEM((n_sup, n_tgt), F32), pltpu.VMEM((n_sup, n_sup), F32),
             pltpu.VMEM((n_sup, n_tgt), F32), pltpu.VMEM((n_sup, n_tgt), F32), pltpu.VMEM((n_sup, n_tgt), F32),
-            pltpu.VMEM((n_sup, n_tgt), BF16),
+            pltpu.VMEM((2, n_sup, n_tgt), BF16),
             pltpu.VMEM((128, n_sup), F32), pltpu.VMEM((n_sup, 128), F32),
             pltpu.VMEM((LAYERS, 8, n_tgt), F32), pltpu.VMEM((n_tgt, 128), F32),
             pltpu.VMEM((n_sup, n_sup), F32), pltpu.VMEM((n_sup, 128), F32),
+            pltpu.SemaphoreType.DMA((32,)),
         ],
         compiler_params=pltpu.CompilerParams(vmem_limit_bytes=56 * 2**20),
         name="compute",
     )(lab_s, lab_t, gathered, target_images)
 
 
-def finish_kernel(sup, grad_own, total, inv, system, coef_t, coef_n, own_tg, own_tr, out, loss):
+def finish_kernel(gathered, images, grad_own, total, inv, system, coef_t, coef_n, own_tg, own_tr, out, loss, sup, sems):
+    copies = load_images(gathered, sup, sems)
     n_sup = sup.shape[0]
-    own_rows = grad_own.shape[0]
+    own_rows = grad_own.shape[1]
     start = pl.multiple_of(lax.axis_index("sup") * own_rows, 8)
     own = pl.ds(start, own_rows)
     lane = lax.broadcasted_iota(jnp.int32, (n_sup, CLS), 1)
@@ -325,38 +354,313 @@
     slab_own = total[own, :]
     d_norm = jnp.sum(d_kern * own_tr[...], axis=1, keepdims=True)
     d_norm = d_norm + jnp.sum(jnp.where(lane == C + 1, slab_own, 0.0), axis=1, keepdims=True)
-    loss[...] = jnp.where(lane == C, slab_own, 0.0)
+    loss[...] = jnp.where(lane == C, total[:own_rows, :], 0.0)
     high, low = split(weight)
+    for copy in copies:
+        copy.wait()
     for k in range(D // 512):
         lanes = slice(k * 512, (k + 1) * 512)
         part = dot(high, sup[:, lanes]) + dot(low, sup[:, lanes])
-        part = part + grad_own[:, lanes].astype(F32)
-        part = part + (2.0 / D) * d_norm * sup[own, lanes].astype(F32)
+        h, shift = divmod(k, D // 1024)
+        part = part + grad_own[h, :, shift * 512:(shift + 1) * 512]
+        part = part + (2.0 / D) * d_norm * images[:, lanes].astype(F32)
         out[:, lanes] = n_sup * part
 
 
-def finish(gathered, grad_own, total, inv, system, coef_t, coef_n, own_tg, own_tr):
-    own_rows = grad_own.shape[0]
+def finish(gathered, images, grad_own, total, inv, system, coef_t, coef_n, own_tg, own_tr):
+    own_rows = grad_own.shape[1]
     vmem = pl.BlockSpec(memory_space=pltpu.VMEM)
     return pl.pallas_call(
         finish_kernel,
         out_shape=[jax.ShapeDtypeStruct((own_rows, D), F32), jax.ShapeDtypeStruct((own_rows, CLS), F32)],
-        in_specs=[vmem] * 9,
+        in_specs=[pl.BlockSpec(memory_space=pl.ANY)] + [vmem] * 9,
         out_specs=[vmem] * 2,
+        scratch_shapes=[pltpu.VMEM((inv.shape[0], D), BF16), pltpu.SemaphoreType.DMA((32,))],
         compiler_params=pltpu.CompilerParams(vmem_limit_bytes=48 * 2**20),
         name="finish",
-    )(gathered, grad_own, total, inv, system, coef_t, coef_n, own_tg, own_tr)
+    )(gathered, images, grad_own, total, inv, system, coef_t, coef_n, own_tg, own_tr)
+
+
+MESH = pl.DeviceIdType.MESH
+RING = 4
+
+
+def place():
+    tgt, sup = lax.axis_index("tgt"), lax.axis_index("sup")
+    core = tgt % 2
+    zh = sup % RING
+    x = (sup // RING) % RING
+    y = sup // (RING * RING)
+    a = y + core * (x - y)
+    b = x + core * (y - x)
+    step_a, step_b = RING - (RING - 1) * core, 1 + (RING - 1) * core
+
+    def device(a_there, b_there, zh_there):
+        return (tgt, (a_there * step_a + b_there * step_b) * RING + zh_there)
+
+    partner = (tgt + 1 - 2 * core, sup)
+    beside = ((tgt + 2) % 4, sup)
+    return core, y, x, a, b, zh, device, partner, beside
+
+
+def turn(index, by):
+    return (index + by) % RING
+
+
+def greet(devices):
+    barrier = pltpu.get_barrier_semaphore()
+    for device in devices:
+        pl.semaphore_signal(barrier, inc=1, device_id=device, device_id_type=MESH)
+    pl.semaphore_wait(barrier, len(devices))
+
+
+class Sender:
+    def __init__(self, send_sems, recv_sems):
+        self.send_sems, self.recv_sems, self.made = send_sems, recv_sems, []
+
+    def start(self, src, dst, device):
+        k = len(self.made)
+        copy = pltpu.make_async_remote_copy(
+            src_ref=src, dst_ref=dst, send_sem=self.send_sems.at[k], recv_sem=self.recv_sems.at[k],
+            device_id=device, device_id_type=MESH)
+        copy.start()
+        self.made.append(copy)
+        return copy
+
+    def drain(self):
+        for copy in self.made:
+            copy.wait_send()
+
+
+def ring_gather(sender, block, me, left, right, then=None):
+    then = then or (lambda ref: None)
+    low, high = pl.ds(0, 2), pl.ds(2, 2)
+    to_right = sender.start(block(me), block(me), right)
+    to_left = sender.start(block(me), block(me), left)
+    to_right.wait_recv()
+    before = block(turn(me, 3))
+    far_right = sender.start(before.at[low], before.at[low], right)
+    to_left.wait_recv()
+    after = block(turn(me, 1))
+    far_left = sender.start(after.at[high], after.at[high], left)
+    then(before)
+    then(after)
+    far = block(turn(me, 2))
+    far_right.wait_recv()
+    then(far.at[low])
+    far_left.wait_recv()
+    then(far.at[high])
+
+
+def gather_kernel(own, out, send_sems, recv_sems, local_sem):
+    core, y, x, a, b, zh, device, partner, beside = place()
+    greet(
+        [device(a, b, turn(zh, k)) for k in (1, 2, 3)]
+        + [device(a, turn(b, k), zh) for k in (1, 3)] + [device(turn(a, k), b, zh) for k in (1, 3)] + [partner]
+    )
+    half = out.shape[-1]
+    mine = own.at[:, pl.ds(pl.multiple_of(core * half, 128), half)]
+    sender = Sender(send_sems, recv_sems)
+    first = [sender.start(mine, out.at[core, a, b, zh], device(a, b, turn(zh, k))) for k in (1, 3, 2)]
+    local = pltpu.make_async_copy(mine, out.at[core, a, b, zh], local_sem)
+    local.start()
+    local.wait()
+    for copy in first:
+        copy.wait_recv()
+    ring_gather(sender, lambda i: out.at[core, a, i], b, device(a, turn(b, 3), zh), device(a, turn(b, 1), zh))
+    across = []
+
+    def share(ref):
+        across.append(sender.start(ref, ref, partner))
+
+    share(out.at[core, a])
+    ring_gather(sender, lambda i: out.at[core, i], a, device(turn(a, 3), b, zh), device(turn(a, 1), b, zh), share)
+    for copy in across:
+        copy.wait_recv()
+    sender.drain()
+
+
+def gather_images(support_images):
+    rows = support_images.shape[0]
+    return pl.pallas_call(
+        gather_kernel,
+        out_shape=jax.ShapeDtypeStruct((2, RING, RING, RING, rows, D // 2), BF16),
+        in_specs=[pl.BlockSpec(memory_space=pl.ANY)],
+        out_specs=pl.BlockSpec(memory_space=pl.ANY),
+        scratch_shapes=[pltpu.SemaphoreType.DMA((16,)), pltpu.SemaphoreType.DMA((16,)), pltpu.SemaphoreType.DMA],
+        compiler_params=pltpu.CompilerParams(collective_id=0, has_side_effects=True),
+        name="gather",
+    )(support_images)
+
+
+def add_blocks(dst, parts, lead):
+    count = math.prod(lead)
+
+    def one(t, carry):
+        index = []
+        for length in reversed(lead):
+            index.append(t % length)
+            t = t // length
+        index = tuple(reversed(index))
+        total = dst[index].astype(F32)
+        for part in parts:
+            total = total + part[index].astype(F32)
+        dst[index] = total.astype(dst.dtype)
+        return carry
+
+    lax.fori_loop(0, count, one, 0)
+
+
+class Scatter:
+    def __init__(self, source, work, near_a, far_a, near_b, far_b, tail, near_z, ends, sender):
+        self.source, self.work, self.near_a, self.far_a = source, work, near_a, far_a
+        self.near_b, self.far_b, self.tail, self.near_z = near_b, far_b, tail, near_z
+        self.ends, self.sender = ends, sender
+
+
+def ring_scatter_start(array, near, block, me, left, right):
+    far = block(turn(me, 2))
+    to_right = array.sender.start(far.at[pl.ds(0, 2)], near.at[0], right)
+    to_left = array.sender.start(far.at[pl.ds(2, 2)], near.at[1], left)
+    return to_right, to_left
+
+
+def ring_scatter_middle(array, near, landing, block, me, left, right, copies, lead):
+    to_right, to_left = copies
+    after, before = block(turn(me, 1)), block(turn(me, 3))
+    to_right.wait_recv()
+    add_blocks(after.at[pl.ds(0, 2)], [near.at[0]], (2,) + lead)
+    second_right = array.sender.start(after, landing.at[0], right)
+    to_left.wait_recv()
+    add_blocks(before.at[pl.ds(2, 2)], [near.at[1]], (2,) + lead)
+    second_left = array.sender.start(before, landing.at[1], left)
+    return second_right, second_left
+
+
+def scatter_kernel(grad, slab, out_grad, out_slab, *scratch):
+    core, y, x, a, b, zh, device, partner, beside = place()
+    greet(
+        [device(a, b, turn(zh, k)) for k in (1, 2, 3)]
+        + [device(a, turn(b, k), zh) for k in (1, 3)] + [device(turn(a, k), b, zh) for k in (1, 3)] + [partner, beside]
+    )
+    sems = scratch[-4:]
+    arrays = [
+        Scatter(slab, *scratch[8:16], Sender(sems[2], sems[3])),
+        Scatter(grad, *scratch[0:8], Sender(sems[0], sems[1])),
+    ]
+    left_a, right_a = device(turn(a, 3), b, zh), device(turn(a, 1), b, zh)
+    left_b, right_b = device(a, turn(b, 3), zh), device(a, turn(b, 1), zh)
+    order = (2, 1, 3, 0)
+    pair = {}
+    for k in order:
+        for n, array in enumerate(arrays):
+            there = turn(b, k)
+            pair[n, k] = array.sender.start(array.source.at[1 - core, there], array.work.at[there], partner)
+    first, second = {}, {}
+    for k in order:
+        for n, array in enumerate(arrays):
+            pair[n, k].wait_recv()
+            here = turn(a, k)
+            add_blocks(array.work.at[here], [array.source.at[core, here]], (RING, RING))
+            if k == 2:
+                first[n] = ring_scatter_start(array, array.near_a, lambda i: array.work.at[i], a, left_a, right_a)
+        if k == 3:
+            for n, array in enumerate(arrays):
+                second[n] = ring_scatter_middle(
+                    array, array.near_a, array.far_a, lambda i: array.work.at[i], a, left_a, right_a, first[n], (RING,))
+    for n, array in enumerate(arrays):
+        for copy in second[n]:
+            copy.wait_recv()
+        add_blocks(array.work.at[a], [array.far_a.at[0], array.far_a.at[1]], (RING, RING))
+        first[n] = ring_scatter_start(array, array.near_b, lambda i: array.work.at[a, i], b, left_b, right_b)
+    for n, array in enumerate(arrays):
+        second[n] = ring_scatter_middle(
+            array, array.near_b, array.far_b, lambda i: array.work.at[a, i], b, left_b, right_b, first[n], ())
+    third = {}
+    for n, array in enumerate(arrays):
+        for copy in second[n]:
+            copy.wait_recv()
+        for i in range(RING):
+            array.tail[i] = (
+                array.work[a, b, i].astype(F32) + array.far_b[0, i].astype(F32) + array.far_b[1, i].astype(F32))
+        third[n] = [
+            array.sender.start(array.tail.at[turn(zh, k)], array.near_z.at[k - 1], device(a, b, turn(zh, k)))
+            for k in (2, 1, 3)]
+    fourth = {}
+    for n, array in enumerate(arrays):
+        for copy in third[n]:
+            copy.wait_recv()
+        array.ends[0] = array.tail[zh] + array.near_z[0] + (array.near_z[1] + array.near_z[2])
+        fourth[n] = array.sender.start(array.ends.at[0], array.ends.at[1], beside)
+    slab_a, grad_a = arrays
+    fourth[0].wait_recv()
+    slab_a.ends[2] = slab_a.ends[0] + slab_a.ends[1]
+    swap = slab_a.sender.start(slab_a.ends.at[2], slab_a.ends.at[3], partner)
+    fourth[1].wait_recv()
+    out_grad[core] = grad_a.ends[0] + grad_a.ends[1]
+    last = grad_a.sender.start(out_grad.at[core], out_grad.at[core], partner)
+    swap.wait_recv()
+    out_slab[y, x, zh] = jnp.where(core == 0, slab_a.ends[2], slab_a.ends[3])
+    sender = slab_a.sender
+    spot = out_slab.at[y, x, zh]
+    ring_z = [sender.start(spot, spot, device(a, b, turn(zh, k))) for k in (2, 1, 3)]
+    for copy in ring_z:
+        copy.wait_recv()
+
+    def at_x(k):
+        return (lax.axis_index("tgt"), (y * RING + turn(x, k)) * RING + zh)
+
+    def at_y(k):
+        return (lax.axis_index("tgt"), (turn(y, k) * RING + x) * RING + zh)
+
+    ring_gather(sender, lambda i: out_slab.at[y, i], x, at_x(3), at_x(1))
+    ring_gather(sender, lambda i: out_slab.at[i], y, at_y(3), at_y(1))
+    last.wait_recv()
+    for array in arrays:
+        array.sender.drain()
+
+
+def scatter_sums(grad, slab, rows):
+    def buffers(lanes, dtype):
+        return [
+            pltpu.VMEM((RING, RING, RING, rows, lanes), dtype),
+            pltpu.VMEM((2, 2, RING, rows, lanes), dtype),
+            pltpu.VMEM((2, RING, RING, rows, lanes), dtype),
+            pltpu.VMEM((2, 2, rows, lanes), dtype),
+            pltpu.VMEM((2, RING, rows, lanes), dtype),
+            pltpu.VMEM((RING, rows, lanes), F32),
+            pltpu.VMEM((3, rows, lanes), F32),
+            pltpu.VMEM((4, rows, lanes), F32),
+        ]
+
+    vmem = pl.BlockSpec(memory_space=pltpu.VMEM)
+    half = D // 2
+    return pl.pallas_call(
+        scatter_kernel,
+        out_shape=[
+            jax.ShapeDtypeStruct((2, rows, half), F32),
+            jax.ShapeDtypeStruct((RING, RING, RING, rows, CLS), F32),
+        ],
+        in_specs=[vmem] * 2,
+        out_specs=[vmem] * 2,
+        scratch_shapes=buffers(half, BF16) + buffers(CLS, F32) + [
+            pltpu.SemaphoreType.DMA((20,)), pltpu.SemaphoreType.DMA((20,)),
+            pltpu.SemaphoreType.DMA((32,)), pltpu.SemaphoreType.DMA((32,)),
+        ],
+        compiler_params=pltpu.CompilerParams(
+            collective_id=1, has_side_effects=True, vmem_limit_bytes=40 * 2**20),
+        name="scatter",
+    )(grad.reshape(2, RING, RING, RING, rows, half), slab.reshape(2, RING, RING, RING, rows, CLS))
 
 
 def body(support_images, target_images, support_labels, target_labels):
     own_rows = support_images.shape[0]
     lab_s = support_labels.reshape(1, -1)
     lab_t = target_labels.reshape(1, -1)
-    gathered = lax.all_gather(support_images, "sup", axis=0, tiled=True)
-    grad, slab, *rest = compute(gathered, target_images, lab_s, lab_t, own_rows, F32)
-    total = lax.psum(slab, ("tgt", "sup"))
-    grad_own = lax.psum(lax.psum_scatter(grad, "sup", scatter_dimension=0, tiled=True), "tgt")
-    out, loss = finish(gathered, grad_own, total, *rest)
+    gathered = gather_images(support_images).reshape(2, RING * RING, RING * own_rows, D // 2)
+    grad, slab, *rest = compute(gathered, target_images, lab_s, lab_t, own_rows)
+    grad_own, total = scatter_sums(grad, slab, own_rows)
+    out, loss = finish(gathered, support_images, grad_own, total.reshape(-1, CLS), *rest)
     return out, jnp.sum(loss[0])
 
 

time: 750 us -> 191 us (0.25)
  the two profiles are of different devices: /device:TPU:1 before, /device:TPU:10 now
where the time goes in v2:
time: 191 us
  Pallas kernels  184 us (96%)
  local copies, waits for them, and re-layouts  6.25 us (3%)
    pallas_call x1, Pallas kernels, compute(): pl.pallas_call(compute_kernel, out_shape=[jax.ShapeDtypeStruct(s, t) for...  76.7 us
    pallas_call x1, Pallas kernels, scatter_sums(): pl.pallas_call(scatter_kernel, out_shape=[jax.ShapeDtypeStruct((2, rows,...  56.8 us
    pallas_call x1, Pallas kernels, gather_images(): pl.pallas_call(gather_kernel, out_shape=jax.ShapeDtypeStruct((2, RING, RI...  35.5 us
    pallas_call x1, Pallas kernels, finish(): pl.pallas_call(finish_kernel, out_shape=[jax.ShapeDtypeStruct((own_rows,...  14.6 us
    unnamed x20, local copies, waits for them, and re-layouts  6.25 us

profile of v2, /device:TPU:10, one launch (start us, length us, event | category | flops | bytes accessed | tf_op | source)
XLA Modules:
  0.0 191.2 jit_solution(8078741093855087436)
XLA Ops:
  0.6 35.5 %gather.1 = bf16[2,4,4,4,8,1536]{5,4,3,2,1,0:T(8,128)(2,1)} custom-call(bf16[8,3072]{1,0:T(8,128)(2,1)} %images.1), custom_call_target="tpu_custom_call" | custom-call | tf_op jit(solution)/shard_map/gather/pallas_call | solution.py:485
  36.1 0.0 copy-start.7
  36.1 76.7 %compute.1 = (bf16[2,512,1536]{2,1,0:T(8,128)(2,1)}, f32[2,512,128]{2,1,0:T(8,128)}, f32[512,512]{1,0:T(8,128)}, f32[512,512]{1,0:T(8,128)}, f32[128,512]{1,0:T(...) custom-call(s32[1,512]{1,0:T(1,128)} %bitcast.12, s32[1,1024]{1,0:T(1,128)} %bitcast.11, ...), custom_call_target="tpu_custom_call" | custom-call | tf_op jit(solution)/shard_map/compute/pallas_call | solution.py:311
  112.9 0.0 copy-start
  112.9 0.0 copy-start.1
  112.9 2.0 %copy-done.1 = bf16[2,512,1536]{2,1,0:T(8,128)(2,1)S(1)} copy-done((bf16[2,512,1536]{2,1,0:T(8,128)(2,1)S(1)}, bf16[2,512,1536]{2,1,0:T(8,128)(2,1)}, u32[]{:S(2)}) %copy-start.1) | copy-done | bytes 3145752
  114.9 0.0 copy-start.4
  114.9 1.0 copy-done.4
  116.0 0.0 copy-start.5
  116.0 0.0 copy-start.6
  116.0 0.0 copy-start.8
  116.0 56.8 %scatter.1 = (f32[2,8,1536]{2,1,0:T(8,128)S(1)}, f32[4,4,4,8,128]{4,3,2,1,0:T(8,128)S(1)}) custom-call(bf16[2,4,4,4,8,1536]{5,4,3,2,1,0:T(8,128)(2,1)S(1)} %bitcast.8, f32[2,4,4,4,8,128]{5,4,3,2,1,0:T(8,128)S(1)} %bitcast.9), custom_call_target="tpu_custom_call" | custom-call | tf_op jit(solution)/shard_map/scatter/pallas_call | solution.py:638
  172.8 0.0 copy-done.7
  172.8 0.0 copy-done
  172.8 0.0 copy-done.5
  172.8 0.0 copy-done.6
  172.8 0.0 copy-done.8
  172.8 0.0 copy-start.2
  172.8 1.2 copy-done.2
  174.1 0.0 copy-start.3
  174.1 1.2 copy-done.3
  175.3 0.0 copy-start.9
  175.3 0.7 copy-done.9
  176.0 14.6 %finish.1 = (f32[8,3072]{1,0:T(8,128)}, f32[8,128]{1,0:T(8,128)S(1)}) custom-call(bf16[2,16,32,1536]{3,2,1,0:T(8,128)(2,1)S(1)} %bitcast.7, bf16[8,3072]{1,0:T(8,128)(2,1)S(1)} %copy-done.7, f32[2,8,1536]{2,1,0:T(8,128)S(1)} %get-tuple-element.16.grad_own, f32[512,128]{1,0:T(8,128)S(1)} %bitcast.10, f32[512,512]{1,0:T(8,128)S(1)} %copy-done.2, ...), custom_call_target="tpu_custom_call" | custom-call | tf_op jit(solution)/shard_map/finish/pallas_call | solution.py:373
  190.6 0.6 slice_reduce_fusion
Async XLA Ops:
  36.1 136.7 %copy-start.7 = (bf16[8,3072]{1,0:T(8,128)(2,1)S(1)}, bf16[8,3072]{1,0:T(8,128)(2,1)}, u32[]{:S(2)}) copy-start(bf16[8,3072]{1,0:T(8,128)(2,1)} %images.1) | copy-start | bytes 147460
  112.9 59.9 %copy-start = (bf16[2,4,4,4,8,1536]{5,4,3,2,1,0:T(8,128)(2,1)S(1)}, bf16[2,4,4,4,8,1536]{5,4,3,2,1,0:T(8,128)(2,1)}, u32[]{:S(2)}) copy-start(bf16[2,4,4,4,8,1536]{5,4,3,2,1,0:T(8,128)(2,1)} %gather.1) | copy-start | bytes 9437188
  112.9 2.0 %copy-start.1 = (bf16[2,512,1536]{2,1,0:T(8,128)(2,1)S(1)}, bf16[2,512,1536]{2,1,0:T(8,128)(2,1)}, u32[]{:S(2)}) copy-start(bf16[2,512,1536]{2,1,0:T(8,128)(2,1)} %get-tuple-element.14) | copy-start | bytes 9437188
  114.9 1.0 copy-start.4
  116.0 56.8 %copy-start.5 = (f32[128,512]{1,0:T(8,128)S(1)}, f32[128,512]{1,0:T(8,128)}, u32[]{:S(2)}) copy-start(f32[128,512]{1,0:T(8,128)} %get-tuple-element.20.coef_t) | copy-start | bytes 786436
  116.0 56.8 %copy-start.6 = (f32[512,128]{1,0:T(8,128)S(1)}, f32[512,128]{1,0:T(8,128)}, u32[]{:S(2)}) copy-start(f32[512,128]{1,0:T(8,128)} %get-tuple-element.21.coef_n) | copy-start | bytes 786436
  116.0 56.8 %copy-start.8 = (f32[8,512]{1,0:T(8,128)S(1)}, f32[8,512]{1,0:T(8,128)}, u32[]{:S(2)}) copy-start(f32[8,512]{1,0:T(8,128)} %get-tuple-element.22.own_tg) | copy-start | bytes 49156
  172.8 1.2 copy-start.2
  174.1 1.2 copy-start.3
  175.3 0.7 copy-start.9

commit v3 on v2

--- a/solution.py
+++ b/solution.py
@@ -15,7 +15,7 @@
 RIDGE = 0.1
 TWO_PI = 2.0 / math.pi
 NEWTON = 7
-REFINE = 3
+REFINE = 2
 HI = lax.Precision.HIGHEST
 NN = (((1,), (0,)), ((), ()))
 NT = (((1,), (1,)), ((), ()))
@@ -184,14 +184,14 @@
     quant_t[...] = quant[...].T
 
     def ss_tile(i, carry):
-        rows = pl.ds(pl.multiple_of(i * 8, 8), 8)
+        rows = pl.ds(pl.multiple_of(i * 32, 32), 32)
         q = quant_t[rows, :]
         left = [q[:, l * 8:l * 8 + 1] for l in range(LAYERS)]
-        right = [quant[l * 8:l * 8 + 8, :] for l in range(LAYERS)]
+        right = [quant[l * 8:l * 8 + 1, :] for l in range(LAYERS)]
         system[rows, :] = ntk_value(gram_ss[rows, :], left, right)
         return carry
 
-    lax.fori_loop(0, n_sup // 8, ss_tile, 0)
+    lax.fori_loop(0, n_sup // 32, ss_tile, 0)
     def own_tile(i, carry):
         here = pl.ds(pl.multiple_of(i * 8, 8), 8)
         own = pl.ds(pl.multiple_of(lax.axis_index("sup") * own_rows + i * 8, 8), 8)
@@ -222,7 +222,7 @@
         tr_s[rows, lanes] = tr
         return carry
 
-    lax.fori_loop(0, (n_sup // 8) * (n_tgt // half), ts_tile, 0)
+    lax.fori_loop(0, (n_sup // 8) * (n_tgt // half), ts_tile, 0, unroll=2)
 
     kern_ss = system[...]
     trace = jnp.sum(jnp.sum(jnp.where(diagonal, kern_ss, 0.0), axis=0, keepdims=True), axis=1, keepdims=True)
@@ -328,59 +328,6 @@
     )(lab_s, lab_t, gathered, target_images)
 
 
-def finish_kernel(gathered, images, grad_own, total, inv, system, coef_t, coef_n, own_tg, own_tr, out, loss, sup, sems):
-    copies = load_images(gathered, sup, sems)
-    n_sup = sup.shape[0]
-    own_rows = grad_own.shape[1]
-    start = pl.multiple_of(lax.axis_index("sup") * own_rows, 8)
-    own = pl.ds(start, own_rows)
-    lane = lax.broadcasted_iota(jnp.int32, (n_sup, CLS), 1)
-    d_coef = jnp.where(lane < C, total[...], 0.0)
-    adjoint = dot(inv[...], d_coef, NN, HI)
-    for k in range(REFINE):
-        left_over = d_coef - dot(system[...], adjoint, NN, HI)
-        adjoint = adjoint + dot(inv[...], left_over, NN, HI)
-    coefs = coef_n[...]
-    ridge = jnp.sum(jnp.sum(adjoint * coefs, axis=0, keepdims=True), axis=1, keepdims=True) * (-RIDGE / n_sup)
-    row_id = lax.broadcasted_iota(jnp.int32, (own_rows, n_sup), 0) + start
-    col_id = lax.broadcasted_iota(jnp.int32, (own_rows, n_sup), 1)
-    mine = row_id == col_id
-    pick = jnp.where(mine, 1.0, 0.0)
-    adj_own = dot(pick, adjoint, NN, HI)
-    d_kern = jnp.where(mine, 2.0 * ridge, 0.0) - dot(adj_own, coef_t[...], NN, HI)
-    d_kern = d_kern - dot(coef_n[own, :], adjoint, NT, HI)
-    weight = d_kern * own_tg[...] * (1.0 / D)
-    lane = lax.broadcasted_iota(jnp.int32, (own_rows, CLS), 1)
-    slab_own = total[own, :]
-    d_norm = jnp.sum(d_kern * own_tr[...], axis=1, keepdims=True)
-    d_norm = d_norm + jnp.sum(jnp.where(lane == C + 1, slab_own, 0.0), axis=1, keepdims=True)
-    loss[...] = jnp.where(lane == C, total[:own_rows, :], 0.0)
-    high, low = split(weight)
-    for copy in copies:
-        copy.wait()
-    for k in range(D // 512):
-        lanes = slice(k * 512, (k + 1) * 512)
-        part = dot(high, sup[:, lanes]) + dot(low, sup[:, lanes])
-        h, shift = divmod(k, D // 1024)
-        part = part + grad_own[h, :, shift * 512:(shift + 1) * 512]
-        part = part + (2.0 / D) * d_norm * images[:, lanes].astype(F32)
-        out[:, lanes] = n_sup * part
-
-
-def finish(gathered, images, grad_own, total, inv, system, coef_t, coef_n, own_tg, own_tr):
-    own_rows = grad_own.shape[1]
-    vmem = pl.BlockSpec(memory_space=pltpu.VMEM)
-    return pl.pallas_call(
-        finish_kernel,
-        out_shape=[jax.ShapeDtypeStruct((own_rows, D), F32), jax.ShapeDtypeStruct((own_rows, CLS), F32)],
-        in_specs=[pl.BlockSpec(memory_space=pl.ANY)] + [vmem] * 9,
-        out_specs=[vmem] * 2,
-        scratch_shapes=[pltpu.VMEM((inv.shape[0], D), BF16), pltpu.SemaphoreType.DMA((32,))],
-        compiler_params=pltpu.CompilerParams(vmem_limit_bytes=48 * 2**20),
-        name="finish",
-    )(gathered, images, grad_own, total, inv, system, coef_t, coef_n, own_tg, own_tr)
-
-
 MESH = pl.DeviceIdType.MESH
 RING = 4
 
@@ -512,145 +459,220 @@
 
 
 class Scatter:
-    def __init__(self, source, work, near_a, far_a, near_b, far_b, tail, near_z, ends, sender):
-        self.source, self.work, self.near_a, self.far_a = source, work, near_a, far_a
-        self.near_b, self.far_b, self.tail, self.near_z = near_b, far_b, tail, near_z
-        self.ends, self.sender = ends, sender
-
-
-def ring_scatter_start(array, near, block, me, left, right):
+    def __init__(self, mine, work, near_a, far_a, near_b, far_b, tail, near_z, ends):
+        self.mine, self.work, self.near_a, self.far_a = mine, work, near_a, far_a
+        self.near_b, self.far_b, self.tail, self.near_z, self.ends = near_b, far_b, tail, near_z, ends
+
+
+def ring_scatter_start(sender, near, block, me, left, right):
     far = block(turn(me, 2))
-    to_right = array.sender.start(far.at[pl.ds(0, 2)], near.at[0], right)
-    to_left = array.sender.start(far.at[pl.ds(2, 2)], near.at[1], left)
+    to_right = sender.start(far.at[pl.ds(0, 2)], near.at[0], right)
+    to_left = sender.start(far.at[pl.ds(2, 2)], near.at[1], left)
     return to_right, to_left
 
 
-def ring_scatter_middle(array, near, landing, block, me, left, right, copies, lead):
+def ring_scatter_middle(sender, near, landing, block, me, left, right, copies, lead):
     to_right, to_left = copies
     after, before = block(turn(me, 1)), block(turn(me, 3))
     to_right.wait_recv()
     add_blocks(after.at[pl.ds(0, 2)], [near.at[0]], (2,) + lead)
-    second_right = array.sender.start(after, landing.at[0], right)
+    second_right = sender.start(after, landing.at[0], right)
     to_left.wait_recv()
     add_blocks(before.at[pl.ds(2, 2)], [near.at[1]], (2,) + lead)
-    second_left = array.sender.start(before, landing.at[1], left)
+    second_left = sender.start(before, landing.at[1], left)
     return second_right, second_left
 
 
-def scatter_kernel(grad, slab, out_grad, out_slab, *scratch):
+def receive(copies):
+    for copy in copies:
+        copy.wait_recv()
+
+
+def finish_kernel(
+    grad, slab, inv_hbm, system_hbm, gathered, images, coef_t, coef_n, own_tg, own_tr,
+    out, loss,
+    mine, work, near_a, far_a, near_b, far_b, tail, near_z, ends, done,
+    sum_own, sum_work, sum_a, sum_b, sum_z, sum_all, total, adjoint,
+    inv, system, sup, part,
+    send_sems, recv_sems, sum_send, sum_recv, load_sems, sup_sems,
+):
     core, y, x, a, b, zh, device, partner, beside = place()
+    tgt_id = lax.axis_index("tgt")
+    place_z = zh * 2 + tgt_id // 2
+
+    def along_z(k):
+        there = (place_z + k) % 8
+        return ((there % 2) * 2 + core, (y * RING + x) * RING + there // 2)
+
+    rows = images.shape[0]
+    n_sup = inv.shape[0]
+    half = D // 2
+    loads = [
+        pltpu.make_async_copy(slab.at[core, :, :, pl.ds(2 * core, 2)], sum_own, load_sems.at[0]),
+        pltpu.make_async_copy(grad.at[core], mine, load_sems.at[1]),
+        pltpu.make_async_copy(inv_hbm, inv, load_sems.at[2]),
+        pltpu.make_async_copy(system_hbm, system, load_sems.at[3]),
+    ]
+    for copy in loads:
+        copy.start()
+    images_in = load_images(gathered, sup, sup_sems)
     greet(
-        [device(a, b, turn(zh, k)) for k in (1, 2, 3)]
-        + [device(a, turn(b, k), zh) for k in (1, 3)] + [device(turn(a, k), b, zh) for k in (1, 3)] + [partner, beside]
+        [device(turn(a, k), b, zh) for k in (1, 2, 3)] + [device(a, turn(b, k), zh) for k in (1, 2, 3)]
+        + [along_z(k) for k in range(1, 8)] + [partner]
     )
-    sems = scratch[-4:]
-    arrays = [
-        Scatter(slab, *scratch[8:16], Sender(sems[2], sems[3])),
-        Scatter(grad, *scratch[0:8], Sender(sems[0], sems[1])),
-    ]
+    sums = Sender(sum_send, sum_recv)
+    sender = Sender(send_sems, recv_sems)
     left_a, right_a = device(turn(a, 3), b, zh), device(turn(a, 1), b, zh)
     left_b, right_b = device(a, turn(b, 3), zh), device(a, turn(b, 1), zh)
-    order = (2, 1, 3, 0)
+
+    pair_sum = sums.start(slab.at[1 - core, :, :, pl.ds(2 - 2 * core, 2)], sum_work, partner)
     pair = {}
-    for k in order:
-        for n, array in enumerate(arrays):
-            there = turn(b, k)
-            pair[n, k] = array.sender.start(array.source.at[1 - core, there], array.work.at[there], partner)
-    first, second = {}, {}
-    for k in order:
-        for n, array in enumerate(arrays):
-            pair[n, k].wait_recv()
-            here = turn(a, k)
-            add_blocks(array.work.at[here], [array.source.at[core, here]], (RING, RING))
-            if k == 2:
-                first[n] = ring_scatter_start(array, array.near_a, lambda i: array.work.at[i], a, left_a, right_a)
-        if k == 3:
-            for n, array in enumerate(arrays):
-                second[n] = ring_scatter_middle(
-                    array, array.near_a, array.far_a, lambda i: array.work.at[i], a, left_a, right_a, first[n], (RING,))
-    for n, array in enumerate(arrays):
-        for copy in second[n]:
-            copy.wait_recv()
-        add_blocks(array.work.at[a], [array.far_a.at[0], array.far_a.at[1]], (RING, RING))
-        first[n] = ring_scatter_start(array, array.near_b, lambda i: array.work.at[a, i], b, left_b, right_b)
-    for n, array in enumerate(arrays):
-        second[n] = ring_scatter_middle(
-            array, array.near_b, array.far_b, lambda i: array.work.at[a, i], b, left_b, right_b, first[n], ())
-    third = {}
-    for n, array in enumerate(arrays):
-        for copy in second[n]:
-            copy.wait_recv()
-        for i in range(RING):
-            array.tail[i] = (
-                array.work[a, b, i].astype(F32) + array.far_b[0, i].astype(F32) + array.far_b[1, i].astype(F32))
-        third[n] = [
-            array.sender.start(array.tail.at[turn(zh, k)], array.near_z.at[k - 1], device(a, b, turn(zh, k)))
-            for k in (2, 1, 3)]
-    fourth = {}
-    for n, array in enumerate(arrays):
-        for copy in third[n]:
-            copy.wait_recv()
-        array.ends[0] = array.tail[zh] + array.near_z[0] + (array.near_z[1] + array.near_z[2])
-        fourth[n] = array.sender.start(array.ends.at[0], array.ends.at[1], beside)
-    slab_a, grad_a = arrays
-    fourth[0].wait_recv()
-    slab_a.ends[2] = slab_a.ends[0] + slab_a.ends[1]
-    swap = slab_a.sender.start(slab_a.ends.at[2], slab_a.ends.at[3], partner)
-    fourth[1].wait_recv()
-    out_grad[core] = grad_a.ends[0] + grad_a.ends[1]
-    last = grad_a.sender.start(out_grad.at[core], out_grad.at[core], partner)
-    swap.wait_recv()
-    out_slab[y, x, zh] = jnp.where(core == 0, slab_a.ends[2], slab_a.ends[3])
-    sender = slab_a.sender
-    spot = out_slab.at[y, x, zh]
-    ring_z = [sender.start(spot, spot, device(a, b, turn(zh, k))) for k in (2, 1, 3)]
-    for copy in ring_z:
-        copy.wait_recv()
-
-    def at_x(k):
-        return (lax.axis_index("tgt"), (y * RING + turn(x, k)) * RING + zh)
-
-    def at_y(k):
-        return (lax.axis_index("tgt"), (turn(y, k) * RING + x) * RING + zh)
-
-    ring_gather(sender, lambda i: out_slab.at[y, i], x, at_x(3), at_x(1))
-    ring_gather(sender, lambda i: out_slab.at[i], y, at_y(3), at_y(1))
+    for k in (2, 1, 3, 0):
+        there = turn(b, k)
+        pair[k] = sender.start(grad.at[1 - core, there], work.at[there], partner)
+
+    def add_pair(k):
+        pair[k].wait_recv()
+        here = turn(a, k)
+        add_blocks(work.at[here], [mine.at[here]], (RING, RING))
+
+    def at_a(i):
+        return work.at[i]
+
+    def at_b(i):
+        return work.at[a, i]
+
+    loads[0].wait()
+    pair_sum.wait_recv()
+    add_blocks(sum_work, [sum_own], (RING, RING, 2))
+    hop = [sums.start(sum_work.at[turn(a, k)], sum_a.at[k - 1], device(turn(a, k), b, zh)) for k in (2, 1, 3)]
+    loads[1].wait()
+    add_pair(2)
+    first = ring_scatter_start(sender, near_a, at_a, a, left_a, right_a)
+    receive(hop)
+    add_blocks(sum_work.at[a], [sum_a.at[0], sum_a.at[1], sum_a.at[2]], (RING, 2))
+    hop = [sums.start(sum_work.at[a, turn(b, k)], sum_b.at[k - 1], device(a, turn(b, k), zh)) for k in (2, 1, 3)]
+    add_pair(1)
+    add_pair(3)
+    receive(hop)
+    sum_z[place_z] = sum_work[a, b] + sum_b[0] + sum_b[1] + sum_b[2]
+    hop = [sums.start(sum_z.at[place_z], sum_z.at[place_z], along_z(k)) for k in range(1, 8)]
+    second = ring_scatter_middle(sender, near_a, far_a, at_a, a, left_a, right_a, first, (RING,))
+    receive(hop)
+    whole = sum_z[0]
+    for k in range(1, 8):
+        whole = whole + sum_z[k]
+    sum_all[core, a, b] = whole
+    spot = sum_all.at[core, a, b]
+    hop = [sums.start(spot, spot, device(a, turn(b, k), zh)) for k in (2, 1, 3)]
+    add_pair(0)
+    receive(hop)
+    spot = sum_all.at[core, a]
+    hop = [sums.start(spot, spot, device(turn(a, k), b, zh)) for k in (2, 1, 3)]
+    receive(hop)
+    spot = sum_all.at[core]
+    pair_sum = sums.start(spot, spot, partner)
+    receive(second)
+    add_blocks(work.at[a], [far_a.at[0], far_a.at[1]], (RING, RING))
+    first = ring_scatter_start(sender, near_b, at_b, b, left_b, right_b)
+    pair_sum.wait_recv()
+
+    for i in range(RING):
+        for j in range(RING):
+            base = 4 * rows * (i * RING + j)
+            total[base:base + 2 * rows, :] = sum_all[0, i, j].reshape(2 * rows, CLS)
+            total[base + 2 * rows:base + 4 * rows, :] = sum_all[1, j, i].reshape(2 * rows, CLS)
+    loads[2].wait()
+    loads[3].wait()
+    lane = lax.broadcasted_iota(jnp.int32, (n_sup, CLS), 1)
+    adjoint[...] = dot(inv[...], jnp.where(lane < C, total[...], 0.0), NN, HI)
+    second = ring_scatter_middle(sender, near_b, far_b, at_b, b, left_b, right_b, first, ())
+    left_over = jnp.where(lane < C, total[...], 0.0) - dot(system[...], adjoint[...], NN, HI)
+    adjoint[...] = adjoint[...] + dot(inv[...], left_over, NN, HI)
+    receive(second)
+    for i in range(RING):
+        tail[i] = work[a, b, i].astype(F32) + far_b[0, i].astype(F32) + far_b[1, i].astype(F32)
+    third = [sender.start(tail.at[turn(zh, k)], near_z.at[k - 1], device(a, b, turn(zh, k))) for k in (2, 1, 3)]
+    for k in range(REFINE - 1):
+        left_over = jnp.where(lane < C, total[...], 0.0) - dot(system[...], adjoint[...], NN, HI)
+        adjoint[...] = adjoint[...] + dot(inv[...], left_over, NN, HI)
+    receive(third)
+    ends[0] = tail[zh] + near_z[0] + (near_z[1] + near_z[2])
+    fourth = sender.start(ends.at[0], ends.at[1], beside)
+
+    start = pl.multiple_of(lax.axis_index("sup") * rows, 8)
+    own = pl.ds(start, rows)
+    adj = adjoint[...]
+    ridge = jnp.sum(jnp.sum(adj * coef_n[...], axis=0, keepdims=True), axis=1, keepdims=True) * (-RIDGE / n_sup)
+    row_id = lax.broadcasted_iota(jnp.int32, (rows, n_sup), 0) + start
+    col_id = lax.broadcasted_iota(jnp.int32, (rows, n_sup), 1)
+    d_kern = jnp.where(row_id == col_id, 2.0 * ridge, 0.0) - dot(adjoint[own, :], coef_t[...], NN, HI)
+    d_kern = d_kern - dot(coef_n[own, :], adj, NT, HI)
+    weight = d_kern * own_tg[...] * (1.0 / D)
+    lane = lax.broadcasted_iota(jnp.int32, (rows, CLS), 1)
+    d_norm = jnp.sum(d_kern * own_tr[...], axis=1, keepdims=True)
+    d_norm = d_norm + jnp.sum(jnp.where(lane == C + 1, total[own, :], 0.0), axis=1, keepdims=True)
+    loss[...] = jnp.sum(jnp.where(lane[0:1] == C, total[0:1, :], 0.0), axis=1, keepdims=True)
+    high, low = split(weight)
+    fourth.wait_recv()
+    done[core] = ends[0] + ends[1]
+    last = sender.start(done.at[core], done.at[core], partner)
+    for copy in images_in:
+        copy.wait()
+    for k in range(D // 512):
+        lanes = slice(k * 512, (k + 1) * 512)
+        some = dot(high, sup[:, lanes]) + dot(low, sup[:, lanes])
+        part[:, lanes] = some + (2.0 / D) * d_norm * images[:, lanes].astype(F32)
     last.wait_recv()
-    for array in arrays:
-        array.sender.drain()
-
-
-def scatter_sums(grad, slab, rows):
-    def buffers(lanes, dtype):
-        return [
-            pltpu.VMEM((RING, RING, RING, rows, lanes), dtype),
-            pltpu.VMEM((2, 2, RING, rows, lanes), dtype),
-            pltpu.VMEM((2, RING, RING, rows, lanes), dtype),
-            pltpu.VMEM((2, 2, rows, lanes), dtype),
-            pltpu.VMEM((2, RING, rows, lanes), dtype),
-            pltpu.VMEM((RING, rows, lanes), F32),
-            pltpu.VMEM((3, rows, lanes), F32),
-            pltpu.VMEM((4, rows, lanes), F32),
-        ]
-
+    for h in range(2):
+        lanes = slice(h * half, (h + 1) * half)
+        out[:, lanes] = n_sup * (part[:, lanes] + done[h])
+    sums.drain()
+    sender.drain()
+
+
+def finish(grad, slab, inv, system, gathered, images, coef_t, coef_n, own_tg, own_tr):
+    rows, half, n_sup = images.shape[0], D // 2, inv.shape[0]
     vmem = pl.BlockSpec(memory_space=pltpu.VMEM)
-    half = D // 2
+    hbm = pl.BlockSpec(memory_space=pltpu.HBM)
     return pl.pallas_call(
-        scatter_kernel,
-        out_shape=[
-            jax.ShapeDtypeStruct((2, rows, half), F32),
-            jax.ShapeDtypeStruct((RING, RING, RING, rows, CLS), F32),
-        ],
-        in_specs=[vmem] * 2,
+        finish_kernel,
+        out_shape=[jax.ShapeDtypeStruct((rows, D), F32), jax.ShapeDtypeStruct((1, 1), F32)],
+        in_specs=[hbm] * 5 + [vmem] * 5,
         out_specs=[vmem] * 2,
-        scratch_shapes=buffers(half, BF16) + buffers(CLS, F32) + [
+        scratch_shapes=[
+            pltpu.VMEM((RING, RING, RING, rows, half), BF16),
+            pltpu.VMEM((RING, RING, RING, rows, half), BF16),
+            pltpu.VMEM((2, 2, RING, rows, half), BF16),
+            pltpu.VMEM((2, RING, RING, rows, half), BF16),
+            pltpu.VMEM((2, 2, rows, half), BF16),
+            pltpu.VMEM((2, RING, rows, half), BF16),
+            pltpu.VMEM((RING, rows, half), F32),
+            pltpu.VMEM((3, rows, half), F32),
+            pltpu.VMEM((2, rows, half), F32),
+            pltpu.VMEM((2, rows, half), F32),
+            pltpu.VMEM((RING, RING, 2, rows, CLS), F32),
+            pltpu.VMEM((RING, RING, 2, rows, CLS), F32),
+            pltpu.VMEM((3, RING, 2, rows, CLS), F32),
+            pltpu.VMEM((3, 2, rows, CLS), F32),
+            pltpu.VMEM((8, 2, rows, CLS), F32),
+            pltpu.VMEM((2, RING, RING, 2, rows, CLS), F32),
+            pltpu.VMEM((n_sup, CLS), F32),
+            pltpu.VMEM((n_sup, CLS), F32),
+            pltpu.VMEM((n_sup, n_sup), F32),
+            pltpu.VMEM((n_sup, n_sup), F32),
+            pltpu.VMEM((n_sup, D), BF16),
+            pltpu.VMEM((rows, D), F32),
             pltpu.SemaphoreType.DMA((20,)), pltpu.SemaphoreType.DMA((20,)),
-            pltpu.SemaphoreType.DMA((32,)), pltpu.SemaphoreType.DMA((32,)),
+            pltpu.SemaphoreType.DMA((24,)), pltpu.SemaphoreType.DMA((24,)),
+            pltpu.SemaphoreType.DMA((4,)), pltpu.SemaphoreType.DMA((32,)),
         ],
         compiler_params=pltpu.CompilerParams(
-            collective_id=1, has_side_effects=True, vmem_limit_bytes=40 * 2**20),
-        name="scatter",
-    )(grad.reshape(2, RING, RING, RING, rows, half), slab.reshape(2, RING, RING, RING, rows, CLS))
+            collective_id=1, has_side_effects=True, vmem_limit_bytes=48 * 2**20),
+        name="finish",
+    )(
+        grad.reshape(2, RING, RING, RING, rows, half), slab.reshape(2, RING, RING, RING, rows, CLS),
+        inv, system, gathered, images, coef_t, coef_n, own_tg, own_tr)
 
 
 def body(support_images, target_images, support_labels, target_labels):
@@ -658,10 +680,9 @@
     lab_s = support_labels.reshape(1, -1)
     lab_t = target_labels.reshape(1, -1)
     gathered = gather_images(support_images).reshape(2, RING * RING, RING * own_rows, D // 2)
-    grad, slab, *rest = compute(gathered, target_images, lab_s, lab_t, own_rows)
-    grad_own, total = scatter_sums(grad, slab, own_rows)
-    out, loss = finish(gathered, support_images, grad_own, total.reshape(-1, CLS), *rest)
-    return out, jnp.sum(loss[0])
+    grad, slab, inv, system, *rest = compute(gathered, target_images, lab_s, lab_t, own_rows)
+    out, loss = finish(grad, slab, inv, system, gathered, support_images, *rest)
+    return out, loss[0, 0]
 
 
 def solution(mesh):

time: 191 us -> 162 us (0.85)
  the two profiles are of different devices: /device:TPU:10 before, /device:TPU:1 now
where the time goes in v3:
time: 162 us
  Pallas kernels  152 us (94%)
  local copies, waits for them, and re-layouts  7.47 us (5%)
  between operations  2.45 us (2%)
    pallas_call x1, Pallas kernels, compute(): pl.pallas_call(compute_kernel, out_shape=[jax.ShapeDtypeStruct(s, t) for...  66.7 us
    pallas_call x1, Pallas kernels, finish(): pl.pallas_call(finish_kernel, out_shape=[jax.ShapeDtypeStruct((rows, D),...  47.2 us
    pallas_call x1, Pallas kernels, gather_images(): pl.pallas_call(gather_kernel, out_shape=jax.ShapeDtypeStruct((2, RING, RI...  37.8 us
    unnamed x17, local copies, waits for them, and re-layouts  7.47 us

profile of v3, /device:TPU:1, one launch (start us, length us, event | category | flops | bytes accessed | tf_op | source)
XLA Modules:
  0.0 161.7 jit_solution(15974827195608942857)
XLA Ops:
  0.6 37.8 %gather.1 = bf16[2,4,4,4,8,1536]{5,4,3,2,1,0:T(8,128)(2,1)} custom-call(bf16[8,3072]{1,0:T(8,128)(2,1)} %images.1), custom_call_target="tpu_custom_call" | custom-call | tf_op jit(solution)/shard_map/gather/pallas_call | solution.py:432
  38.4 0.0 copy-start.5
  38.4 66.7 %compute.1 = (bf16[2,512,1536]{2,1,0:T(8,128)(2,1)}, f32[2,512,128]{2,1,0:T(8,128)}, f32[512,512]{1,0:T(8,128)}, f32[512,512]{1,0:T(8,128)}, f32[128,512]{1,0:T(...) custom-call(s32[1,512]{1,0:T(1,128)} %bitcast.11, s32[1,1024]{1,0:T(1,128)} %bitcast.10, ...), custom_call_target="tpu_custom_call" | custom-call | tf_op jit(solution)/shard_map/compute/pallas_call | solution.py:311
  105.2 0.0 copy-done.5
  105.2 0.0 copy-start
  105.2 1.2 copy-done
  106.4 0.0 copy-start.1
  106.4 1.2 copy-done.1
  107.6 0.0 copy-start.2
  107.6 1.0 copy-done.2
  108.7 0.0 copy-start.3
  108.7 0.9 copy-done.3
  109.6 0.0 copy-start.4
  109.6 0.9 copy-done.4
  110.6 0.0 copy-start.6
  110.6 0.7 copy-done.6
  111.3 0.0 copy-start.7
  111.3 0.7 copy-done.7
  112.0 47.2 %finish.1 = (f32[8,3072]{1,0:T(8,128)S(1)}, f32[1,1]{1,0:T(1,128)}) custom-call(bf16[2,4,4,4,8,1536]{5,4,3,2,1,0:T(8,128)(2,1)} %bitcast.9, f32[2,4,4,4,8,128]{5,4,3,2,1,0:T(8,128)S(1)} %bitcast.6, f32[512,512]{1,0:T(8,128)S(1)} %copy-done, f32[512,512]{1,0:T(8,128)S(1)} %copy-done.1, bf16[2,16,32,1536]{3,2,1,0:T(8,128)(2,1)} %bitcast.8, ...), custom_call_target="tpu_custom_call" | custom-call | tf_op jit(solution)/shard_map/finish/pallas_call | solution.py:638
  159.3 0.6 copy.8
Async XLA Ops:
  38.4 66.7 %copy-start.5 = (bf16[8,3072]{1,0:T(8,128)(2,1)S(1)}, bf16[8,3072]{1,0:T(8,128)(2,1)}, u32[]{:S(2)}) copy-start(bf16[8,3072]{1,0:T(8,128)(2,1)} %images.1) | copy-start | bytes 147460
  105.2 1.2 copy-start
  106.4 1.2 copy-start.1
  107.6 1.0 copy-start.2
  108.7 0.9 copy-start.3
  109.6 0.9 copy-start.4
  110.6 0.7 copy-start.6
  111.3 0.7 copy-start.7

commit v4 on v3

--- a/solution.py
+++ b/solution.py
@@ -15,6 +15,7 @@
 RIDGE = 0.1
 TWO_PI = 2.0 / math.pi
 NEWTON = 7
+NEWTON_TILES = 9
 REFINE = 2
 HI = lax.Precision.HIGHEST
 NN = (((1,), (0,)), ((), ()))
@@ -206,24 +207,6 @@
 
     lax.fori_loop(0, own_rows // 8, own_tile, 0)
 
-    half = 512
-
-    def ts_tile(t, carry):
-        i, j = t // (n_tgt // half), t % (n_tgt // half)
-        rows = pl.ds(pl.multiple_of(i * 8, 8), 8)
-        lanes = pl.ds(pl.multiple_of(j * half, half), half)
-        q = quant_t[rows, :]
-        right = [q[:, l * 8:l * 8 + 1] for l in range(LAYERS)]
-        slope = [q[:, 64 + l * 8:65 + l * 8] for l in range(LAYERS)]
-        left2 = [left_s[l, :, lanes] for l in range(LAYERS)]
-        theta, tg, tr = ntk_full(gram[rows, lanes], left2, right, slope)
-        kern[rows, lanes] = theta
-        tg_s[rows, lanes] = tg
-        tr_s[rows, lanes] = tr
-        return carry
-
-    lax.fori_loop(0, (n_sup // 8) * (n_tgt // half), ts_tile, 0, unroll=2)
-
     kern_ss = system[...]
     trace = jnp.sum(jnp.sum(jnp.where(diagonal, kern_ss, 0.0), axis=0, keepdims=True), axis=1, keepdims=True)
     inv_t = n_sup / trace
@@ -236,7 +219,27 @@
     inv[...] = (gain * alpha) * (jnp.where(diagonal, 2.0, 0.0) - alpha * system[...])
     rho = 0.5 * gain * rho * rho
 
+    half = 512
+
+    def ts_tile(i, j):
+        rows = pl.ds(pl.multiple_of(i * 8, 8), 8)
+        lanes = pl.ds(j * half, half)
+        q = quant_t[rows, :]
+        right = [q[:, l * 8:l * 8 + 1] for l in range(LAYERS)]
+        slope = [q[:, 64 + l * 8:65 + l * 8] for l in range(LAYERS)]
+        left2 = [left_s[l, :, lanes] for l in range(LAYERS)]
+        theta, tg, tr = ntk_full(gram[rows, lanes], left2, right, slope)
+        kern[rows, lanes] = theta
+        tg_s[rows, lanes] = tg
+        tr_s[rows, lanes] = tr
+
+
+    each = NEWTON_TILES
+
     def newton(k, rho):
+        for i in range(each):
+            for j in range(n_tgt // half):
+                ts_tile(k * each + i, j)
         a = split(system[...])
         x = split(inv[...])
         mid[...] = jnp.where(diagonal, 2.0, 0.0) - dot3(a, x)
@@ -245,6 +248,13 @@
         return 0.5 * gain * rho * rho
 
     lax.fori_loop(0, NEWTON, newton, rho)
+
+    def ts_rest(i, carry):
+        for j in range(n_tgt // half):
+            ts_tile(i, j)
+        return carry
+
+    lax.fori_loop(NEWTON * each, n_sup // 8, ts_rest, 0)
     inv[...] = inv[...] * inv_t
     system[...] = system[...] * (trace * (1.0 / n_sup))
 
@@ -323,7 +333,7 @@
             pltpu.VMEM((n_sup, n_sup), F32), pltpu.VMEM((n_sup, 128), F32),
             pltpu.SemaphoreType.DMA((32,)),
         ],
-        compiler_params=pltpu.CompilerParams(vmem_limit_bytes=56 * 2**20),
+        compiler_params=pltpu.CompilerParams(vmem_limit_bytes=36 * 2**20),
         name="compute",
     )(lab_s, lab_t, gathered, target_images)
 
@@ -377,26 +387,6 @@
     def drain(self):
         for copy in self.made:
             copy.wait_send()
-
-
-def ring_gather(sender, block, me, left, right, then=None):
-    then = then or (lambda ref: None)
-    low, high = pl.ds(0, 2), pl.ds(2, 2)
-    to_right = sender.start(block(me), block(me), right)
-    to_left = sender.start(block(me), block(me), left)
-    to_right.wait_recv()
-    before = block(turn(me, 3))
-    far_right = sender.start(before.at[low], before.at[low], right)
-    to_left.wait_recv()
-    after = block(turn(me, 1))
-    far_left = sender.start(after.at[high], after.at[high], left)
-    then(before)
-    then(after)
-    far = block(turn(me, 2))
-    far_right.wait_recv()
-    then(far.at[low])
-    far_left.wait_recv()
-    then(far.at[high])
 
 
 def gather_kernel(own, out, send_sems, recv_sems, local_sem):
@@ -414,14 +404,53 @@
     local.wait()
     for copy in first:
         copy.wait_recv()
-    ring_gather(sender, lambda i: out.at[core, a, i], b, device(a, turn(b, 3), zh), device(a, turn(b, 1), zh))
+    low, high = pl.ds(0, 2), pl.ds(2, 2)
+    left_a, right_a = device(turn(a, 3), b, zh), device(turn(a, 1), b, zh)
+    left_b, right_b = device(a, turn(b, 3), zh), device(a, turn(b, 1), zh)
     across = []
 
     def share(ref):
         across.append(sender.start(ref, ref, partner))
 
-    share(out.at[core, a])
-    ring_gather(sender, lambda i: out.at[core, i], a, device(turn(a, 3), b, zh), device(turn(a, 1), b, zh), share)
+    def block(k, m):
+        return out.at[core, turn(a, k), turn(b, m)]
+
+    def send(ref, there):
+        return sender.start(ref, ref, there)
+
+    along_a = {}
+
+    def launch(m):
+        along_a[m] = (send(block(0, m), right_a), send(block(0, m), left_a))
+
+    b_right, b_left = send(block(0, 0), right_b), send(block(0, 0), left_b)
+    launch(0)
+    share(block(0, 0))
+    b_right.wait_recv()
+    far_right = send(block(0, 3).at[low], right_b)
+    launch(3)
+    share(block(0, 3))
+    b_left.wait_recv()
+    far_left = send(block(0, 1).at[high], left_b)
+    launch(1)
+    share(block(0, 1))
+    far_right.wait_recv()
+    far_left.wait_recv()
+    launch(2)
+    share(block(0, 2))
+    last = {}
+    for m in (0, 3, 1, 2):
+        to_right, to_left = along_a[m]
+        to_right.wait_recv()
+        first_half = send(block(3, m).at[low], right_a)
+        share(block(3, m))
+        to_left.wait_recv()
+        last[m] = (first_half, send(block(1, m).at[high], left_a))
+        share(block(1, m))
+    for m in (0, 3, 1, 2):
+        for copy in last[m]:
+            copy.wait_recv()
+        share(block(2, m))
     for copy in across:
         copy.wait_recv()
     sender.drain()
@@ -434,8 +463,10 @@
         out_shape=jax.ShapeDtypeStruct((2, RING, RING, RING, rows, D // 2), BF16),
         in_specs=[pl.BlockSpec(memory_space=pl.ANY)],
         out_specs=pl.BlockSpec(memory_space=pl.ANY),
-        scratch_shapes=[pltpu.SemaphoreType.DMA((16,)), pltpu.SemaphoreType.DMA((16,)), pltpu.SemaphoreType.DMA],
-        compiler_params=pltpu.CompilerParams(collective_id=0, has_side_effects=True),
+        scratch_shapes=[pltpu.SemaphoreType.DMA((40,)), pltpu.SemaphoreType.DMA((40,)), pltpu.SemaphoreType.DMA],
+        compiler_params=pltpu.CompilerParams(
+            collective_id=0, has_side_effects=True, vmem_limit_bytes=4 * 2**20),
+        cost_estimate=pl.CostEstimate(flops=0, bytes_accessed=80 * 2**20, transcendentals=0),
         name="gather",
     )(support_images)
 
@@ -449,6 +480,9 @@
             index.append(t % length)
             t = t // length
         index = tuple(reversed(index))
+        if len(parts) == 1:
+            dst[index] = dst[index] + parts[0][index]
+            return carry
         total = dst[index].astype(F32)
         for part in parts:
             total = total + part[index].astype(F32)
@@ -456,12 +490,6 @@
         return carry
 
     lax.fori_loop(0, count, one, 0)
-
-
-class Scatter:
-    def __init__(self, mine, work, near_a, far_a, near_b, far_b, tail, near_z, ends):
-        self.mine, self.work, self.near_a, self.far_a = mine, work, near_a, far_a
-        self.near_b, self.far_b, self.tail, self.near_z, self.ends = near_b, far_b, tail, near_z, ends
 
 
 def ring_scatter_start(sender, near, block, me, left, right):
@@ -489,12 +517,12 @@
 
 
 def finish_kernel(
-    grad, slab, inv_hbm, system_hbm, gathered, images, coef_t, coef_n, own_tg, own_tr,
+    grad, slab, inv, system, gathered, images, coef_t, coef_n, own_tg, own_tr,
     out, loss,
-    mine, work, near_a, far_a, near_b, far_b, tail, near_z, ends, done,
-    sum_own, sum_work, sum_a, sum_b, sum_z, sum_all, total, adjoint,
-    inv, system, sup, part,
-    send_sems, recv_sems, sum_send, sum_recv, load_sems, sup_sems,
+    work, near_a, far_a, near_b, far_b, tail, near_z, ends, done,
+    sum_work, sum_a, sum_b, sum_z, sum_all, total, adjoint,
+    sup, part,
+    send_sems, recv_sems, sum_send, sum_recv, sup_sems,
 ):
     core, y, x, a, b, zh, device, partner, beside = place()
     tgt_id = lax.axis_index("tgt")
@@ -507,14 +535,6 @@
     rows = images.shape[0]
     n_sup = inv.shape[0]
     half = D // 2
-    loads = [
-        pltpu.make_async_copy(slab.at[core, :, :, pl.ds(2 * core, 2)], sum_own, load_sems.at[0]),
-        pltpu.make_async_copy(grad.at[core], mine, load_sems.at[1]),
-        pltpu.make_async_copy(inv_hbm, inv, load_sems.at[2]),
-        pltpu.make_async_copy(system_hbm, system, load_sems.at[3]),
-    ]
-    for copy in loads:
-        copy.start()
     images_in = load_images(gathered, sup, sup_sems)
     greet(
         [device(turn(a, k), b, zh) for k in (1, 2, 3)] + [device(a, turn(b, k), zh) for k in (1, 2, 3)]
@@ -534,7 +554,7 @@
     def add_pair(k):
         pair[k].wait_recv()
         here = turn(a, k)
-        add_blocks(work.at[here], [mine.at[here]], (RING, RING))
+        add_blocks(work.at[here], [grad.at[core, here]], (RING, RING))
 
     def at_a(i):
         return work.at[i]
@@ -542,11 +562,9 @@
     def at_b(i):
         return work.at[a, i]
 
-    loads[0].wait()
     pair_sum.wait_recv()
-    add_blocks(sum_work, [sum_own], (RING, RING, 2))
+    add_blocks(sum_work, [slab.at[core, :, :, pl.ds(2 * core, 2)]], (RING, RING, 2))
     hop = [sums.start(sum_work.at[turn(a, k)], sum_a.at[k - 1], device(turn(a, k), b, zh)) for k in (2, 1, 3)]
-    loads[1].wait()
     add_pair(2)
     first = ring_scatter_start(sender, near_a, at_a, a, left_a, right_a)
     receive(hop)
@@ -582,8 +600,6 @@
             base = 4 * rows * (i * RING + j)
             total[base:base + 2 * rows, :] = sum_all[0, i, j].reshape(2 * rows, CLS)
             total[base + 2 * rows:base + 4 * rows, :] = sum_all[1, j, i].reshape(2 * rows, CLS)
-    loads[2].wait()
-    loads[3].wait()
     lane = lax.broadcasted_iota(jnp.int32, (n_sup, CLS), 1)
     adjoint[...] = dot(inv[...], jnp.where(lane < C, total[...], 0.0), NN, HI)
     second = ring_scatter_middle(sender, near_b, far_b, at_b, b, left_b, right_b, first, ())
@@ -634,14 +650,12 @@
 def finish(grad, slab, inv, system, gathered, images, coef_t, coef_n, own_tg, own_tr):
     rows, half, n_sup = images.shape[0], D // 2, inv.shape[0]
     vmem = pl.BlockSpec(memory_space=pltpu.VMEM)
-    hbm = pl.BlockSpec(memory_space=pltpu.HBM)
     return pl.pallas_call(
         finish_kernel,
         out_shape=[jax.ShapeDtypeStruct((rows, D), F32), jax.ShapeDtypeStruct((1, 1), F32)],
-        in_specs=[hbm] * 5 + [vmem] * 5,
+        in_specs=[vmem] * 4 + [pl.BlockSpec(memory_space=pl.ANY)] + [vmem] * 5,
         out_specs=[vmem] * 2,
         scratch_shapes=[
-            pltpu.VMEM((RING, RING, RING, rows, half), BF16),
             pltpu.VMEM((RING, RING, RING, rows, half), BF16),
             pltpu.VMEM((2, 2, RING, rows, half), BF16),
             pltpu.VMEM((2, RING, RING, rows, half), BF16),
@@ -652,23 +666,20 @@
             pltpu.VMEM((2, rows, half), F32),
             pltpu.VMEM((2, rows, half), F32),
             pltpu.VMEM((RING, RING, 2, rows, CLS), F32),
-            pltpu.VMEM((RING, RING, 2, rows, CLS), F32),
             pltpu.VMEM((3, RING, 2, rows, CLS), F32),
             pltpu.VMEM((3, 2, rows, CLS), F32),
             pltpu.VMEM((8, 2, rows, CLS), F32),
             pltpu.VMEM((2, RING, RING, 2, rows, CLS), F32),
             pltpu.VMEM((n_sup, CLS), F32),
             pltpu.VMEM((n_sup, CLS), F32),
-            pltpu.VMEM((n_sup, n_sup), F32),
-            pltpu.VMEM((n_sup, n_sup), F32),
             pltpu.VMEM((n_sup, D), BF16),
             pltpu.VMEM((rows, D), F32),
             pltpu.SemaphoreType.DMA((20,)), pltpu.SemaphoreType.DMA((20,)),
             pltpu.SemaphoreType.DMA((24,)), pltpu.SemaphoreType.DMA((24,)),
-            pltpu.SemaphoreType.DMA((4,)), pltpu.SemaphoreType.DMA((32,)),
+            pltpu.SemaphoreType.DMA((32,)),
         ],
         compiler_params=pltpu.CompilerParams(
-            collective_id=1, has_side_effects=True, vmem_limit_bytes=48 * 2**20),
+            collective_id=1, has_side_effects=True, vmem_limit_bytes=24 * 2**20),
         name="finish",
     )(
         grad.reshape(2, RING, RING, RING, rows, half), slab.reshape(2, RING, RING, RING, rows, CLS),

time: 162 us -> 140 us (0.86)
  Pallas kernels: 152 us -> 133 us
  local copies, waits for them, and re-layouts: 7.47 us -> 4.23 us
    pallas_call x1, Pallas kernels: 66.7 us -> 54.3 us  [compute(): pl.pallas_call(compute_kernel, out_shape=[jax.ShapeDtypeStruct(s, t) for...]
    pallas_call x1, Pallas kernels: 37.8 us -> 32.1 us  [gather_images(): pl.pallas_call(gather_kernel, out_shape=jax.ShapeDtypeStruct((2, RING, RI...]
    unnamed x17 -> x11, local copies, waits for them, and re-layouts: 7.47 us -> 4.23 us
where the time goes in v4:
time: 140 us
  Pallas kernels  133 us (95%)
  local copies, waits for them, and re-layouts  4.23 us (3%)
  between operations  2.52 us (2%)
    pallas_call x1, Pallas kernels, compute(): pl.pallas_call(compute_kernel, out_shape=[jax.ShapeDtypeStruct(s, t) for...  54.3 us
    pallas_call x1, Pallas kernels, finish(): pl.pallas_call(finish_kernel, out_shape=[jax.ShapeDtypeStruct((rows, D),...  47.1 us
    pallas_call x1, Pallas kernels, gather_images(): pl.pallas_call(gather_kernel, out_shape=jax.ShapeDtypeStruct((2, RING, RI...  32.1 us
    unnamed x11, local copies, waits for them, and re-layouts  4.23 us

profile of v4, /device:TPU:1, one launch (start us, length us, event | category | flops | bytes accessed | tf_op | source)
XLA Modules:
  0.0 140.2 jit_solution(5568987570214101241)
XLA Ops:
  0.6 0.0 copy-start.4
  0.6 0.0 copy-start.1
  0.7 0.8 copy-done.1
  1.4 0.0 copy-start.3
  1.4 32.1 %gather.1 = bf16[2,4,4,4,8,1536]{5,4,3,2,1,0:T(8,128)(2,1)S(1)} custom-call(bf16[8,3072]{1,0:T(8,128)(2,1)S(1)} %copy-done.1), custom_call_target="tpu_custom_call" | custom-call | bytes 83886080 | tf_op jit(solution)/shard_map/gather/pallas_call | solution.py:461
  33.5 0.0 copy-done.4
  33.6 0.0 copy-done.3
  33.6 0.0 copy-start
  33.6 2.8 %copy-done = bf16[1024,3072]{1,0:T(8,128)(2,1)S(1)} copy-done((bf16[1024,3072]{1,0:T(8,128)(2,1)S(1)}, bf16[1024,3072]{1,0:T(8,128)(2,1)}, u32[]{:S(2)}) %copy-start) | copy-done | bytes 6291480
  36.4 0.0 copy-start.2
  36.4 54.3 %compute.1 = (bf16[2,512,1536]{2,1,0:T(8,128)(2,1)S(1)}, f32[2,512,128]{2,1,0:T(8,128)S(1)}, f32[512,512]{1,0:T(8,128)S(1)}, f32[512,512]{1,0:T(8,128)S(1)}, f32...) custom-call(s32[1,512]{1,0:T(1,128)S(1)} %bitcast.11, ...), custom_call_target="tpu_custom_call" | custom-call | tf_op jit(solution)/shard_map/compute/pallas_call | solution.py:321
  90.6 0.0 copy-done.2
  90.6 47.1 %finish.1 = (f32[8,3072]{1,0:T(8,128)S(1)}, f32[1,1]{1,0:T(1,128)}) custom-call(bf16[2,4,4,4,8,1536]{5,4,3,2,1,0:T(8,128)(2,1)S(1)} %bitcast.8, f32[2,4,4,4,8,128]{5,4,3,2,1,0:T(8,128)S(1)} %bitcast.9, f32[512,512]{1,0:T(8,128)S(1)} %get-tuple-element.14.inv, f32[512,512]{1,0:T(8,128)S(1)} %get-tuple-element.15.system, ...), custom_call_target="tpu_custom_call" | custom-call | tf_op jit(solution)/shard_map/finish/pallas_call | solution.py:653
  137.8 0.6 copy.8
Async XLA Ops:
  0.6 32.9 %copy-start.4 = (s32[512]{0:T(512)S(1)}, s32[512]{0:T(512)}, u32[]{:S(2)}) copy-start(s32[512]{0:T(512)} %param.6) | copy-start | bytes 6148
  0.6 0.8 copy-start.1
  1.4 32.1 %copy-start.3 = (s32[1024]{0:T(1024)S(1)}, s32[1024]{0:T(1024)}, u32[]{:S(2)}) copy-start(s32[1024]{0:T(1024)} %param.7) | copy-start | bytes 12292
  33.6 2.8 %copy-start = (bf16[1024,3072]{1,0:T(8,128)(2,1)S(1)}, bf16[1024,3072]{1,0:T(8,128)(2,1)}, u32[]{:S(2)}) copy-start(bf16[1024,3072]{1,0:T(8,128)(2,1)} %tgt.1) | copy-start | bytes 18874372
  36.4 54.3 %copy-start.2 = (bf16[8,3072]{1,0:T(8,128)(2,1)S(1)}, bf16[8,3072]{1,0:T(8,128)(2,1)}, u32[]{:S(2)}) copy-start(bf16[8,3072]{1,0:T(8,128)(2,1)} %images.1) | copy-start | bytes 147460

commit v5 on v4

--- a/solution.py
+++ b/solution.py
@@ -25,10 +25,10 @@
 
 ASIN = (
     (1.0, 0.1666678637266159, 0.0749453455209732, 0.0455390103161335, 0.02390936389565468, 0.042553599923849106),
-    (1.0, 0.16666781902313232, 0.07494797557592392, 0.04552660509943962, 0.02313542366027832, 0.0537058524787426, -0.05348314717411995, 0.08573318272829056),
-    (1.0, 0.16666752099990845, 0.07495901733636856, 0.04535885155200958, 0.024863531813025475, 0.04080614075064659),
+    (1.0, 0.1666594296693802, 0.07524710148572922, 0.04152849689126015, 0.04858245328068733, -0.02943584695458412, 0.08121654391288757),
+    (1.0, 0.16665531694889069, 0.07537393271923065, 0.04041983559727669, 0.0488600954413414),
     (1.0, 0.16666492819786072, 0.0750882476568222, 0.043096426874399185, 0.04107564687728882),
-    (1.0, 0.16666613519191742, 0.07503537833690643, 0.043817341327667236, 0.03804752230644226),
+    (0.9999999403953552, 0.16668136417865753, 0.07438473403453827, 0.052717722952365875),
 )
 
 
@@ -89,20 +89,19 @@
         w = lax.rsqrt(1.0 - u2)
         cw2 = c2 * w
         step = TWO_PI * cw2
-        bend = u * (w * cw2)
-        ww = w * w
-        tb = theta * bend
+        tw = theta * (w * w)
+        tb = tw * (u * c2)
         gs = g * slope[layer]
         if layer == 0:
             tg_next = step * (2.0 + tb)
             dg_next = step
             base = -gs
-            tr_next = step * (base - theta * (ww * slope[layer]))
+            tr_next = step * (base - tw * slope[layer])
         else:
             tg_next = step * (dg + tg + tb * dg)
             dg_next = step * dg
             base = gr - gs
-            tr_next = step * (base + tr + (tb * gr - theta * (ww * slope[layer])))
+            tr_next = step * (base + tr + (tb * gr - tw * slope[layer]))
         gr_next = step * base
         g = scaled_asin(layer, u, u2)
         theta = g + step * theta
@@ -389,7 +388,9 @@
             copy.wait_send()
 
 
-def gather_kernel(own, out, send_sems, recv_sems, local_sem):
+def gather_kernel(own, tgt, out, tgt_near, send_sems, recv_sems, local_sem, tgt_sem):
+    near = pltpu.make_async_copy(tgt, tgt_near, tgt_sem)
+    near.start()
     core, y, x, a, b, zh, device, partner, beside = place()
     greet(
         [device(a, b, turn(zh, k)) for k in (1, 2, 3)]
@@ -454,21 +455,26 @@
     for copy in across:
         copy.wait_recv()
     sender.drain()
-
-
-def gather_images(support_images):
+    near.wait()
+
+
+def gather_images(support_images, target_images):
     rows = support_images.shape[0]
     return pl.pallas_call(
         gather_kernel,
-        out_shape=jax.ShapeDtypeStruct((2, RING, RING, RING, rows, D // 2), BF16),
-        in_specs=[pl.BlockSpec(memory_space=pl.ANY)],
-        out_specs=pl.BlockSpec(memory_space=pl.ANY),
-        scratch_shapes=[pltpu.SemaphoreType.DMA((40,)), pltpu.SemaphoreType.DMA((40,)), pltpu.SemaphoreType.DMA],
+        out_shape=[
+            jax.ShapeDtypeStruct((2, RING, RING, RING, rows, D // 2), BF16),
+            jax.ShapeDtypeStruct(target_images.shape, BF16),
+        ],
+        in_specs=[pl.BlockSpec(memory_space=pl.ANY)] * 2,
+        out_specs=[pl.BlockSpec(memory_space=pl.ANY)] * 2,
+        scratch_shapes=[pltpu.SemaphoreType.DMA((40,)), pltpu.SemaphoreType.DMA((40,)), pltpu.SemaphoreType.DMA,
+            pltpu.SemaphoreType.DMA],
         compiler_params=pltpu.CompilerParams(
-            collective_id=0, has_side_effects=True, vmem_limit_bytes=4 * 2**20),
+            collective_id=0, has_side_effects=True, vmem_limit_bytes=41 * 2**20),
         cost_estimate=pl.CostEstimate(flops=0, bytes_accessed=80 * 2**20, transcendentals=0),
         name="gather",
-    )(support_images)
+    )(support_images, target_images)
 
 
 def add_blocks(dst, parts, lead):
@@ -503,10 +509,10 @@
     to_right, to_left = copies
     after, before = block(turn(me, 1)), block(turn(me, 3))
     to_right.wait_recv()
-    add_blocks(after.at[pl.ds(0, 2)], [near.at[0]], (2,) + lead)
+    add_blocks(after.at[pl.ds(0, 2)], [near.at[0]], lead)
     second_right = sender.start(after, landing.at[0], right)
     to_left.wait_recv()
-    add_blocks(before.at[pl.ds(2, 2)], [near.at[1]], (2,) + lead)
+    add_blocks(before.at[pl.ds(2, 2)], [near.at[1]], lead)
     second_left = sender.start(before, landing.at[1], left)
     return second_right, second_left
 
@@ -521,7 +527,7 @@
     out, loss,
     work, near_a, far_a, near_b, far_b, tail, near_z, ends, done,
     sum_work, sum_a, sum_b, sum_z, sum_all, total, adjoint,
-    sup, part,
+    sup, part, pieces,
     send_sems, recv_sems, sum_send, sum_recv, sup_sems,
 ):
     core, y, x, a, b, zh, device, partner, beside = place()
@@ -554,7 +560,7 @@
     def add_pair(k):
         pair[k].wait_recv()
         here = turn(a, k)
-        add_blocks(work.at[here], [grad.at[core, here]], (RING, RING))
+        add_blocks(work.at[here], [grad.at[core, here]], (RING,))
 
     def at_a(i):
         return work.at[i]
@@ -563,19 +569,19 @@
         return work.at[a, i]
 
     pair_sum.wait_recv()
-    add_blocks(sum_work, [slab.at[core, :, :, pl.ds(2 * core, 2)]], (RING, RING, 2))
+    sum_work[...] = sum_work[...] + slab[core, :, :, pl.ds(2 * core, 2)]
     hop = [sums.start(sum_work.at[turn(a, k)], sum_a.at[k - 1], device(turn(a, k), b, zh)) for k in (2, 1, 3)]
     add_pair(2)
     first = ring_scatter_start(sender, near_a, at_a, a, left_a, right_a)
     receive(hop)
-    add_blocks(sum_work.at[a], [sum_a.at[0], sum_a.at[1], sum_a.at[2]], (RING, 2))
+    sum_work[a] = sum_work[a] + sum_a[0] + sum_a[1] + sum_a[2]
     hop = [sums.start(sum_work.at[a, turn(b, k)], sum_b.at[k - 1], device(a, turn(b, k), zh)) for k in (2, 1, 3)]
     add_pair(1)
     add_pair(3)
     receive(hop)
     sum_z[place_z] = sum_work[a, b] + sum_b[0] + sum_b[1] + sum_b[2]
     hop = [sums.start(sum_z.at[place_z], sum_z.at[place_z], along_z(k)) for k in range(1, 8)]
-    second = ring_scatter_middle(sender, near_a, far_a, at_a, a, left_a, right_a, first, (RING,))
+    second = ring_scatter_middle(sender, near_a, far_a, at_a, a, left_a, right_a, first, (2,))
     receive(hop)
     whole = sum_z[0]
     for k in range(1, 8):
@@ -591,8 +597,16 @@
     spot = sum_all.at[core]
     pair_sum = sums.start(spot, spot, partner)
     receive(second)
-    add_blocks(work.at[a], [far_a.at[0], far_a.at[1]], (RING, RING))
+
+    def add_a(k):
+        here = turn(b, k)
+        add_blocks(work.at[a, here], [far_a.at[0, here], far_a.at[1, here]], (RING,))
+
+    add_a(2)
     first = ring_scatter_start(sender, near_b, at_b, b, left_b, right_b)
+    add_a(1)
+    add_a(3)
+    add_a(0)
     pair_sum.wait_recv()
 
     for i in range(RING):
@@ -612,10 +626,6 @@
     for k in range(REFINE - 1):
         left_over = jnp.where(lane < C, total[...], 0.0) - dot(system[...], adjoint[...], NN, HI)
         adjoint[...] = adjoint[...] + dot(inv[...], left_over, NN, HI)
-    receive(third)
-    ends[0] = tail[zh] + near_z[0] + (near_z[1] + near_z[2])
-    fourth = sender.start(ends.at[0], ends.at[1], beside)
-
     start = pl.multiple_of(lax.axis_index("sup") * rows, 8)
     own = pl.ds(start, rows)
     adj = adjoint[...]
@@ -629,16 +639,21 @@
     d_norm = jnp.sum(d_kern * own_tr[...], axis=1, keepdims=True)
     d_norm = d_norm + jnp.sum(jnp.where(lane == C + 1, total[own, :], 0.0), axis=1, keepdims=True)
     loss[...] = jnp.sum(jnp.where(lane[0:1] == C, total[0:1, :], 0.0), axis=1, keepdims=True)
-    high, low = split(weight)
-    fourth.wait_recv()
-    done[core] = ends[0] + ends[1]
-    last = sender.start(done.at[core], done.at[core], partner)
+    pieces[0:rows] = weight
+    pieces[rows:2 * rows] = weight - weight.astype(BF16).astype(F32)
+    both = pieces[...].astype(BF16)
     for copy in images_in:
         copy.wait()
     for k in range(D // 512):
         lanes = slice(k * 512, (k + 1) * 512)
-        some = dot(high, sup[:, lanes]) + dot(low, sup[:, lanes])
-        part[:, lanes] = some + (2.0 / D) * d_norm * images[:, lanes].astype(F32)
+        some = dot(both, sup[:, lanes])
+        part[:, lanes] = some[:rows] + some[rows:] + (2.0 / D) * d_norm * images[:, lanes].astype(F32)
+    receive(third)
+    ends[0] = tail[zh] + near_z[0] + (near_z[1] + near_z[2])
+    fourth = sender.start(ends.at[0], ends.at[1], beside)
+    fourth.wait_recv()
+    done[core] = ends[0] + ends[1]
+    last = sender.start(done.at[core], done.at[core], partner)
     last.wait_recv()
     for h in range(2):
         lanes = slice(h * half, (h + 1) * half)
@@ -674,6 +689,7 @@
             pltpu.VMEM((n_sup, CLS), F32),
             pltpu.VMEM((n_sup, D), BF16),
             pltpu.VMEM((rows, D), F32),
+            pltpu.VMEM((2 * rows, n_sup), F32),
             pltpu.SemaphoreType.DMA((20,)), pltpu.SemaphoreType.DMA((20,)),
             pltpu.SemaphoreType.DMA((24,)), pltpu.SemaphoreType.DMA((24,)),
             pltpu.SemaphoreType.DMA((32,)),
@@ -690,8 +706,9 @@
     own_rows = support_images.shape[0]
     lab_s = support_labels.reshape(1, -1)
     lab_t = target_labels.reshape(1, -1)
-    gathered = gather_images(support_images).reshape(2, RING * RING, RING * own_rows, D // 2)
-    grad, slab, inv, system, *rest = compute(gathered, target_images, lab_s, lab_t, own_rows)
+    gathered, near = gather_images(support_images, target_images)
+    gathered = gathered.reshape(2, RING * RING, RING * own_rows, D // 2)
+    grad, slab, inv, system, *rest = compute(gathered, near, lab_s, lab_t, own_rows)
     out, loss = finish(grad, slab, inv, system, gathered, support_images, *rest)
     return out, loss[0, 0]
 

time: 140 us -> 136 us (0.971)
  local copies, waits for them, and re-layouts: 4.23 us -> 1.45 us
    unnamed x11 -> x7, local copies, waits for them, and re-layouts: 4.23 us -> 1.45 us
where the time goes in v5:
time: 136 us
  Pallas kernels  132 us (97%)
  between operations  2.38 us (2%)
  local copies, waits for them, and re-layouts  1.45 us (1%)
    pallas_call x1, Pallas kernels, compute(): pl.pallas_call(compute_kernel, out_shape=[jax.ShapeDtypeStruct(s, t) for...  53.2 us
    pallas_call x1, Pallas kernels, finish(): pl.pallas_call(finish_kernel, out_shape=[jax.ShapeDtypeStruct((rows, D),...  46.8 us
    pallas_call x1, Pallas kernels, gather_images(): pl.pallas_call(gather_kernel, out_shape=[jax.ShapeDtypeStruct((2, RING, R...  32.1 us

profile of v5, /device:TPU:1, one launch (start us, length us, event | category | flops | bytes accessed | tf_op | source)
XLA Modules:
  0.0 135.9 jit_solution(411791167637337121)
XLA Ops:
  0.6 0.0 copy-start.2
  0.6 0.0 copy-start
  0.6 0.8 copy-done
  1.4 0.0 copy-start.1
  1.4 32.1 %gather.1 = (bf16[2,4,4,4,8,1536]{5,4,3,2,1,0:T(8,128)(2,1)S(1)}, bf16[1024,3072]{1,0:T(8,128)(2,1)S(1)}) custom-call(bf16[8,3072]{1,0:T(8,128)(2,1)S(1)} %copy-done, bf16[1024,3072]{1,0:T(8,128)(2,1)} %tgt.1), custom_call_target="tpu_custom_call" | custom-call | bytes 83886080 | tf_op jit(solution)/shard_map/gather/pallas_call | solution.py:463
  33.6 0.0 copy-done.2
  33.6 0.0 copy-done.1
  33.6 53.2 %compute.1 = (bf16[2,512,1536]{2,1,0:T(8,128)(2,1)S(1)}, f32[2,512,128]{2,1,0:T(8,128)S(1)}, f32[512,512]{1,0:T(8,128)S(1)}, f32[512,512]{1,0:T(8,128)S(1)}, f32...) custom-call(s32[1,512]{1,0:T(1,128)S(1)} %bitcast.11, ...), custom_call_target="tpu_custom_call" | custom-call | tf_op jit(solution)/shard_map/compute/pallas_call | solution.py:320
  86.8 46.8 %finish.1 = (f32[8,3072]{1,0:T(8,128)S(1)}, f32[1,1]{1,0:T(1,128)}) custom-call(bf16[2,4,4,4,8,1536]{5,4,3,2,1,0:T(8,128)(2,1)S(1)} %bitcast.8, f32[2,4,4,4,8,128]{5,4,3,2,1,0:T(8,128)S(1)} %bitcast.9, f32[512,512]{1,0:T(8,128)S(1)} %get-tuple-element.18.inv, f32[512,512]{1,0:T(8,128)S(1)} %get-tuple-element.19.system, ...), custom_call_target="tpu_custom_call" | custom-call | tf_op jit(solution)/shard_map/finish/pallas_call | solution.py:668
  133.6 0.6 copy.8
Async XLA Ops:
  0.6 32.9 %copy-start.2 = (s32[512]{0:T(512)S(1)}, s32[512]{0:T(512)}, u32[]{:S(2)}) copy-start(s32[512]{0:T(512)} %param.6) | copy-start | bytes 6148
  0.6 0.8 copy-start
  1.4 32.1 %copy-start.1 = (s32[1024]{0:T(1024)S(1)}, s32[1024]{0:T(1024)}, u32[]{:S(2)}) copy-start(s32[1024]{0:T(1024)} %param.7) | copy-start | bytes 12292

commit v6 on v5

--- a/solution.py
+++ b/solution.py
@@ -151,27 +151,6 @@
     for j in range(n_sup // 256):
         gram_ss[:, j * 256:(j + 1) * 256] = dot(sup[...], sup[j * 256:(j + 1) * 256, :], NT) * (1.0 / D)
 
-    def gram_tile(j, carry):
-        rows = pl.ds(pl.multiple_of(j * 256, 256), 256)
-        gram[:, rows] = dot(sup[...], tgt[rows, :], NT) * (1.0 / D)
-        return carry
-
-    lax.fori_loop(0, n_tgt // 256, gram_tile, 0)
-
-    def square_tile(j, carry):
-        rows = pl.ds(pl.multiple_of(j * 64, 64), 64)
-        total = jnp.zeros((64, 128), F32)
-        for k in range(D // 128):
-            x = tgt[rows, k * 128:(k + 1) * 128].astype(F32)
-            total = total + x * x
-        sq[rows, :] = total
-        return carry
-
-    lax.fori_loop(0, n_tgt // 64, square_tile, 0)
-    norm_t = dot(jnp.full((8, 128), 1.0 / D, F32), sq[...], NT, HI)
-    scales_t, unused = norm_layers(norm_t)
-    for layer in range(LAYERS):
-        left_s[layer] = 2.0 * scales_t[layer]
     row_id = lax.broadcasted_iota(jnp.int32, (n_sup, n_sup), 0)
     col_id = lax.broadcasted_iota(jnp.int32, (n_sup, n_sup), 1)
     diagonal = row_id == col_id
@@ -183,15 +162,36 @@
         quant[64 + layer * 8:72 + layer * 8, :] = slopes_s[layer]
     quant_t[...] = quant[...].T
 
-    def ss_tile(i, carry):
+    def ss_tile(i):
         rows = pl.ds(pl.multiple_of(i * 32, 32), 32)
         q = quant_t[rows, :]
         left = [q[:, l * 8:l * 8 + 1] for l in range(LAYERS)]
         right = [quant[l * 8:l * 8 + 1, :] for l in range(LAYERS)]
         system[rows, :] = ntk_value(gram_ss[rows, :], left, right)
+
+    def square_tile(j):
+        rows = pl.ds(pl.multiple_of(j * 64, 64), 64)
+        total = jnp.zeros((64, 128), F32)
+        for k in range(D // 128):
+            x = tgt[rows, k * 128:(k + 1) * 128].astype(F32)
+            total = total + x * x
+        sq[rows, :] = total
+
+    def gram_tile(j, carry):
+        rows = pl.ds(pl.multiple_of(j * 256, 256), 256)
+        gram[:, rows] = dot(sup[...], tgt[rows, :], NT) * (1.0 / D)
+        for i in range(4):
+            square_tile(j * 4 + i)
+        for i in range(n_sup // 128):
+            ss_tile(j * (n_sup // 128) + i)
         return carry
 
-    lax.fori_loop(0, n_sup // 32, ss_tile, 0)
+    lax.fori_loop(0, n_tgt // 256, gram_tile, 0)
+    norm_t = dot(jnp.full((8, 128), 1.0 / D, F32), sq[...], NT, HI)
+    scales_t, unused = norm_layers(norm_t)
+    for layer in range(LAYERS):
+        left_s[layer] = 2.0 * scales_t[layer]
+
     def own_tile(i, carry):
         here = pl.ds(pl.multiple_of(i * 8, 8), 8)
         own = pl.ds(pl.multiple_of(lax.axis_index("sup") * own_rows + i * 8, 8), 8)
@@ -505,15 +505,25 @@
     return to_right, to_left
 
 
+def ring_scatter_early(sender, landing, block, me, left, right):
+    after, before = block(turn(me, 1)), block(turn(me, 3))
+    low, high = pl.ds(0, 2), pl.ds(2, 2)
+    return [
+        sender.start(after.at[high], landing.at[0, high], right),
+        sender.start(before.at[low], landing.at[1, low], left),
+    ]
+
+
 def ring_scatter_middle(sender, near, landing, block, me, left, right, copies, lead):
     to_right, to_left = copies
+    low, high = pl.ds(0, 2), pl.ds(2, 2)
     after, before = block(turn(me, 1)), block(turn(me, 3))
     to_right.wait_recv()
     add_blocks(after.at[pl.ds(0, 2)], [near.at[0]], lead)
-    second_right = sender.start(after, landing.at[0], right)
+    second_right = sender.start(after.at[low], landing.at[0, low], right)
     to_left.wait_recv()
     add_blocks(before.at[pl.ds(2, 2)], [near.at[1]], lead)
-    second_left = sender.start(before, landing.at[1], left)
+    second_left = sender.start(before.at[high], landing.at[1, high], left)
     return second_right, second_left
 
 
@@ -578,6 +588,7 @@
     hop = [sums.start(sum_work.at[a, turn(b, k)], sum_b.at[k - 1], device(a, turn(b, k), zh)) for k in (2, 1, 3)]
     add_pair(1)
     add_pair(3)
+    early = ring_scatter_early(sender, far_a, at_a, a, left_a, right_a)
     receive(hop)
     sum_z[place_z] = sum_work[a, b] + sum_b[0] + sum_b[1] + sum_b[2]
     hop = [sums.start(sum_z.at[place_z], sum_z.at[place_z], along_z(k)) for k in range(1, 8)]
@@ -596,6 +607,7 @@
     receive(hop)
     spot = sum_all.at[core]
     pair_sum = sums.start(spot, spot, partner)
+    receive(early)
     receive(second)
 
     def add_a(k):
@@ -606,6 +618,7 @@
     first = ring_scatter_start(sender, near_b, at_b, b, left_b, right_b)
     add_a(1)
     add_a(3)
+    early = ring_scatter_early(sender, far_b, at_b, b, left_b, right_b)
     add_a(0)
     pair_sum.wait_recv()
 
@@ -619,6 +632,7 @@
     second = ring_scatter_middle(sender, near_b, far_b, at_b, b, left_b, right_b, first, ())
     left_over = jnp.where(lane < C, total[...], 0.0) - dot(system[...], adjoint[...], NN, HI)
     adjoint[...] = adjoint[...] + dot(inv[...], left_over, NN, HI)
+    receive(early)
     receive(second)
     for i in range(RING):
         tail[i] = work[a, b, i].astype(F32) + far_b[0, i].astype(F32) + far_b[1, i].astype(F32)
@@ -690,7 +704,7 @@
             pltpu.VMEM((n_sup, D), BF16),
             pltpu.VMEM((rows, D), F32),
             pltpu.VMEM((2 * rows, n_sup), F32),
-            pltpu.SemaphoreType.DMA((20,)), pltpu.SemaphoreType.DMA((20,)),
+            pltpu.SemaphoreType.DMA((24,)), pltpu.SemaphoreType.DMA((24,)),
             pltpu.SemaphoreType.DMA((24,)), pltpu.SemaphoreType.DMA((24,)),
             pltpu.SemaphoreType.DMA((32,)),
         ],

time: 136 us -> 133 us (0.978)
  Pallas kernels: 132 us -> 129 us
    pallas_call x1, Pallas kernels: 53.2 us -> 50.9 us  [compute(): pl.pallas_call(compute_kernel, out_shape=[jax.ShapeDtypeStruct(s, t) for...]
where the time goes in v6:
time: 133 us
  Pallas kernels  129 us (97%)
  between operations  2.38 us (2%)
  local copies, waits for them, and re-layouts  1.45 us (1%)
    pallas_call x1, Pallas kernels, compute(): pl.pallas_call(compute_kernel, out_shape=[jax.ShapeDtypeStruct(s, t) for...  50.9 us
    pallas_call x1, Pallas kernels, finish(): pl.pallas_call(finish_kernel, out_shape=[jax.ShapeDtypeStruct((rows, D),...  45.9 us
    pallas_call x1, Pallas kernels, gather_images(): pl.pallas_call(gather_kernel, out_shape=[jax.ShapeDtypeStruct((2, RING, R...  32.1 us

profile of v6, /device:TPU:1, one launch (start us, length us, event | category | flops | bytes accessed | tf_op | source)
XLA Modules:
  0.0 132.7 jit_solution(11859004938142845524)
XLA Ops:
  0.6 0.0 copy-start.2
  0.6 0.0 copy-start
  0.6 0.8 copy-done
  1.4 0.0 copy-start.1
  1.4 32.1 %gather.1 = (bf16[2,4,4,4,8,1536]{5,4,3,2,1,0:T(8,128)(2,1)S(1)}, bf16[1024,3072]{1,0:T(8,128)(2,1)S(1)}) custom-call(bf16[8,3072]{1,0:T(8,128)(2,1)S(1)} %copy-done, bf16[1024,3072]{1,0:T(8,128)(2,1)} %tgt.1), custom_call_target="tpu_custom_call" | custom-call | bytes 83886080 | tf_op jit(solution)/shard_map/gather/pallas_call | solution.py:463
  33.6 0.0 copy-done.2
  33.6 0.0 copy-done.1
  33.6 50.9 %compute.1 = (bf16[2,512,1536]{2,1,0:T(8,128)(2,1)S(1)}, f32[2,512,128]{2,1,0:T(8,128)S(1)}, f32[512,512]{1,0:T(8,128)S(1)}, f32[512,512]{1,0:T(8,128)S(1)}, f32...) custom-call(s32[1,512]{1,0:T(1,128)S(1)} %bitcast.11, ...), custom_call_target="tpu_custom_call" | custom-call | tf_op jit(solution)/shard_map/compute/pallas_call | solution.py:320
  84.4 45.9 %finish.1 = (f32[8,3072]{1,0:T(8,128)S(1)}, f32[1,1]{1,0:T(1,128)}) custom-call(bf16[2,4,4,4,8,1536]{5,4,3,2,1,0:T(8,128)(2,1)S(1)} %bitcast.8, f32[2,4,4,4,8,128]{5,4,3,2,1,0:T(8,128)S(1)} %bitcast.9, f32[512,512]{1,0:T(8,128)S(1)} %get-tuple-element.18.inv, f32[512,512]{1,0:T(8,128)S(1)} %get-tuple-element.19.system, ...), custom_call_target="tpu_custom_call" | custom-call | tf_op jit(solution)/shard_map/finish/pallas_call | solution.py:682
  130.4 0.6 copy.8
Async XLA Ops:
  0.6 32.9 %copy-start.2 = (s32[512]{0:T(512)S(1)}, s32[512]{0:T(512)}, u32[]{:S(2)}) copy-start(s32[512]{0:T(512)} %param.6) | copy-start | bytes 6148
  0.6 0.8 copy-start
  1.4 32.1 %copy-start.1 = (s32[1024]{0:T(1024)S(1)}, s32[1024]{0:T(1024)}, u32[]{:S(2)}) copy-start(s32[1024]{0:T(1024)} %param.7) | copy-start | bytes 12292
